TPU v7x, 256 devices: a whole 4x4x8 slice. The times are simulated.
256 devices in a mesh: inst: 8 (over y, x_lo), ax: 16 (over z, core), circ: 2 (over x_hi).
Axes of the slice: x: 4 (x_hi: 2, x_lo: 2; x = x_hi * 2 + x_lo), y: 4, z: 8, core: 2. Of those that a mesh axis runs over, the one named last changes fastest.
Arguments:
- flow_state: float32 [8, 7, 128, 128, 128], P('inst', None, 'ax', 'circ'), may hold values from -2 to 40, as said below
- thinc_flags: int32 [8, 128, 128], P('inst', 'ax', 'circ'), may hold values 0 or 1
Outputs:
- new_state: float32 [8, 7, 128, 128, 128], P('inst', None, 'ax', 'circ')
Inputs may be any that keep to these rules, and one draw needn't show every extreme that they name: `flow_state`: every cell holds a two-phase state with positive partial densities and positive pressure, whose seventh field, the volume fraction, lies between 0.02 and 0.98.
All inputs are finite; a program needn't handle non-finite values. No bound on the sum of `thinc_flags` on one device may be relied on, other than what follows from the above.
Results may differ from a plain program's by a relative error of at most 0.0003.
Values sent between devices are 32-bit elements; how exact they have to be, the bound alone decides.
No kernel may reach another device: no remote copies, remote signals or barrier semaphores. Data moves between devices by JAX's collectives and lax.ppermute only.
A program may use at most 64 MiB of HBM per device.

v0:
```python
import functools
import math

import jax
import jax.numpy as jnp
from jax import lax
from jax.experimental import pallas as pl
from jax.experimental.pallas import tpu as pltpu
from jax.sharding import PartitionSpec as P


G_LIQ = 4.4
P_LIQ = 6.0
G_GAS = 1.4
BETA = 1.6
EPSA = 0.1
ALPHA = 4.0
DIAG0 = 0.016
OMEGA = 1.0
NU_T = 0.25

FIELDS = 7
COEFS = 5
TILE = 8
CHUNKS = ((0, 7),)


VMEM = pl.BlockSpec(memory_space=pltpu.VMEM)


def spectral_weights(count):
    table = []
    for k in range(count):
        if k == 0:
            first, second = 0.0, -(count * count + 2) / 12.0
        else:
            sign = 1.0 if k % 2 == 0 else -1.0
            angle = math.pi * k / count
            first = 0.5 * sign * math.cos(angle) / math.sin(angle)
            second = -sign / (2.0 * math.sin(angle) ** 2)
        table.append(OMEGA * first - NU_T * OMEGA * OMEGA * second)
    return table


def call(kernel, outs, *operands, flops=0):
    outs = [jax.ShapeDtypeStruct(shape, jnp.float32) for shape in outs]
    total = sum(x.size * 4 for x in operands) + sum(x.size * 4 for x in outs)
    return pl.pallas_call(
        kernel,
        out_shape=outs,
        in_specs=[VMEM] * len(operands),
        out_specs=[VMEM] * len(outs),
        compiler_params=pltpu.CompilerParams(vmem_limit_bytes=20 << 20),
        cost_estimate=pl.CostEstimate(flops=flops, bytes_accessed=total, transcendentals=0),
    )(*operands)


def spectral_kernel(weights, state_ref, out_ref):
    count, fields, rows, _ = state_ref.shape
    half = count // 2
    even = [0.5 * (weights[k] + weights[k + half]) for k in range(half)]
    odd = [0.5 * (weights[k] - weights[k + half]) for k in range(half)]

    def step(index, _):
        field = index // (rows // TILE)
        span = pl.ds(pl.multiple_of((index % (rows // TILE)) * TILE, TILE), TILE)
        cells = [state_ref[m, field, span] for m in range(count)]
        sums = [cells[m] + cells[m + half] for m in range(half)]
        diffs = [cells[m] - cells[m + half] for m in range(half)]
        for n in range(half):
            total = sum(even[(n - m) % half] * sums[m] for m in range(half))
            alternate = sum(
                (odd[n - m] if n >= m else -odd[n - m + half]) * diffs[m] for m in range(half)
            )
            out_ref[n, field, span] = total + alternate
            out_ref[n + half, field, span] = total - alternate
        return 0

    lax.fori_loop(0, fields * (rows // TILE), step, 0)


def primitives(cells):
    density = cells[0] + cells[1]
    inverse = 1.0 / density
    vel_ax = cells[2] * inverse
    vel_circ = cells[3] * inverse
    vel_rad = cells[4] * inverse
    fraction = cells[6]
    gamma_term = fraction / (G_LIQ - 1.0) + (1.0 - fraction) / (G_GAS - 1.0)
    stiff_term = fraction * (G_LIQ * P_LIQ / (G_LIQ - 1.0))
    kinetic = 0.5 * density * (vel_ax * vel_ax + vel_circ * vel_circ + vel_rad * vel_rad)
    gamma_inv = 1.0 / gamma_term
    pressure = (cells[5] - kinetic - stiff_term) * gamma_inv
    sound_speed = jnp.sqrt(((1.0 + gamma_inv) * pressure + stiff_term * gamma_inv) * inverse)
    return vel_ax, vel_circ, pressure, sound_speed


def sharpen(lower_val, centre, upper_val, offset):
    average = 0.5 * (lower_val + upper_val)
    difference = upper_val - lower_val
    steepness = 2.0 * (centre - average) / (jnp.abs(difference) + EPSA)
    return average + 0.5 * difference * jnp.tanh(BETA * (steepness + offset))


def flux_kernel(state_ref, halo_ref, flag_ref, res_ref, coup_ref, inv_ref, v_ref, w_ref, red_ref):
    planes = state_ref.shape[2]
    rows = state_ref.shape[3]
    last = planes - 1

    def plane(i, _):
        cells = []
        for f in range(FIELDS):
            edge = halo_ref[f, i]
            cells.append(
                jnp.concatenate(
                    [state_ref[0, f, i], edge[0:2], edge[0:2], edge[2:4], edge[2:4]], axis=0
                )
            )
        edge = halo_ref[FIELDS, i]
        flags = jnp.concatenate([flag_ref[i], edge, edge], axis=0)
        total = rows + TILE

        def below(x, by=1):
            return pltpu.roll(x, by, 0)

        def above(x):
            return pltpu.roll(x, total - 1, 0)

        vel_ax, vel_circ, pressure, sound = primitives(cells)
        coup_ref[i] = -ALPHA * (jnp.abs(vel_ax) + sound)[:rows]
        wave = jnp.abs(vel_circ) + sound
        half_speed = 0.5 * jnp.maximum(below(wave), wave)
        fraction = cells[6]
        back1 = below(fraction)
        sharp_left = sharpen(below(fraction, 2), back1, fraction, 1.0)
        sharp_right = sharpen(back1, fraction, above(fraction), -1.0)
        flagged = flags > 0.5
        frac_left = jnp.where(flagged, sharp_left, back1)
        frac_right = jnp.where(flagged, sharp_right, fraction)
        for f in range(FIELDS):
            if f < 6:
                flux = cells[f] * vel_circ
                if f == 3:
                    flux = flux + pressure
                elif f == 5:
                    flux = flux + pressure * vel_circ
                mean = 0.5 * (below(flux) + flux)
                jump = cells[f] - below(cells[f])
            else:
                mean = 0.5 * (frac_left * below(vel_circ) + frac_right * vel_circ)
                jump = frac_right - frac_left
            face = mean - half_speed * jump
            res_ref[i, f] = (above(face) - face)[:rows]
        return 0

    lax.fori_loop(0, planes, plane, 0)

    def factor(t, _):
        span = pl.ds(pl.multiple_of(t * TILE, TILE), TILE)
        coup = [coup_ref[i, span] for i in range(planes)]
        inv, ratio, v = [], [], []
        for i in range(last):
            pivot = DIAG0 - 2.0 * coup[i]
            if i:
                pivot = pivot - coup[i] * ratio[-1]
            inv.append(1.0 / pivot)
            ratio.append(coup[i] * inv[-1])
            v.append(inv[-1] if i == 0 else -(ratio[-1] * v[-1]))
            inv_ref[i, span] = inv[-1]
        v_next, w_next = v[-1], inv[-1]
        v_last, w_last = v_next * coup[0], w_next * coup[last - 1]
        for i in range(last - 1, -1, -1):
            if i < last - 1:
                v_next = v[i] - ratio[i] * v_next
                w_next = -(ratio[i] * w_next)
            v_first, w_first = v_next * coup[0], w_next * coup[last - 1]
            v_ref[i, span] = v_first
            w_ref[i, span] = w_first
        sep = coup[last]
        rows_out = (
            -(sep * v_last),
            DIAG0 - 2.0 * sep - sep * w_last,
            sep,
            v_first,
            w_first,
        )
        for k, value in enumerate(rows_out):
            red_ref[k, span] = value
        return 0

    lax.fori_loop(0, rows // TILE, factor, 0)


def sweep_kernel(first, res_ref, spec_ref, coup_ref, inv_ref, coef_ref, y_ref, red_ref):
    planes, fields, rows, _ = spec_ref.shape
    last = planes - 1

    def step(t, _):
        span = pl.ds(pl.multiple_of(t * TILE, TILE), TILE)
        coup = [coup_ref[i, span] for i in range(planes)]
        inv = [inv_ref[i, span] for i in range(last)]
        ratio = [coup[i] * inv[i] for i in range(last)]
        for f in range(fields):
            value = []
            for i in range(last):
                right = -(res_ref[i, first + f, span] + spec_ref[i, f, span])
                if i:
                    right = right - coup[i] * value[-1]
                value.append(right * inv[i])
            y = value[-1]
            y_last = y
            y_ref[last - 1, f, span] = y
            for i in range(last - 2, -1, -1):
                y = value[i] - ratio[i] * y
                y_ref[i, f, span] = y
            right = -(res_ref[last, first + f, span] + spec_ref[last, f, span])
            own = right - coup[last] * y_last
            for k, x in ((f, y), (fields + f, own)):
                red_ref[2 * t, k] = x[0:4]
                red_ref[2 * t + 1, k] = x[4:8]
        for k in range(COEFS):
            x = coef_ref[k, span]
            red_ref[2 * t, 2 * fields + k] = x[0:4]
            red_ref[2 * t + 1, 2 * fields + k] = x[4:8]
        return 0

    lax.fori_loop(0, rows // TILE, step, 0)


def reduced_kernel(rhs_ref, out_ref):
    count = rhs_ref.shape[0]
    fields = out_ref.shape[1] // 2
    base = 2 * fields
    ratio = []
    values = []
    for p in range(count):
        lower, diag, sep = rhs_ref[p, base], rhs_ref[p, base + 1], rhs_ref[p, base + 2]
        more = p + 1 < count
        if more:
            diag = diag - sep * rhs_ref[p + 1, base + 3]
        if p:
            diag = diag - lower * ratio[-1]
        inv = 1.0 / diag
        if more:
            ratio.append(-(sep * rhs_ref[p + 1, base + 4]) * inv)
        row = []
        for f in range(fields):
            right = rhs_ref[p, fields + f]
            if more:
                right = right - sep * rhs_ref[p + 1, f]
            if p:
                right = right - lower * values[-1][f]
            row.append(right * inv)
        values.append(row)
    solved = values[-1]
    for p in range(count - 1, -1, -1):
        if p < count - 1:
            solved = [values[p][f] - ratio[p] * solved[f] for f in range(fields)]
        for f in range(fields):
            out_ref[p, f] = solved[f]
            if p < count - 1:
                out_ref[p + 1, fields + f] = solved[f]
    for f in range(fields):
        out_ref[0, fields + f] = jnp.zeros_like(solved[f])


def finish_kernel(chunks, state_ref, v_ref, w_ref, *refs):
    out_ref = refs[-1]
    y_refs, sep_refs = refs[: len(chunks)], refs[len(chunks) : 2 * len(chunks)]
    planes, rows = state_ref.shape[2], state_ref.shape[3]
    last = planes - 1

    def step(t, _):
        span = pl.ds(pl.multiple_of(t * TILE, TILE), TILE)
        v = [v_ref[i, span] for i in range(last)]
        w = [w_ref[i, span] for i in range(last)]
        for (first, stop), y_ref, sep_ref in zip(chunks, y_refs, sep_refs):
            fields = stop - first
            for f in range(fields):
                own = jnp.concatenate([sep_ref[2 * t, f], sep_ref[2 * t + 1, f]], axis=0)
                prev = jnp.concatenate(
                    [sep_ref[2 * t, fields + f], sep_ref[2 * t + 1, fields + f]], axis=0
                )
                for i in range(last):
                    delta = y_ref[i, f, span] - v[i] * prev - w[i] * own
                    out_ref[0, first + f, i, span] = state_ref[0, first + f, i, span] + delta
                out_ref[0, first + f, last, span] = state_ref[0, first + f, last, span] + own
        return 0

    lax.fori_loop(0, rows // TILE, step, 0)


def exchange(x, axis):
    return lax.all_to_all(x, axis, 0, 0, tiled=True)


def body(flow_state, thinc_flags):
    own = flow_state[0]
    planes, rows, lanes = own.shape[1:]
    instances = lax.axis_size("inst")
    ax_count = lax.axis_size("ax")
    circ_count = lax.axis_size("circ")
    piece = rows // ax_count
    grid = (rows, lanes)
    weights = spectral_weights(instances)

    flags = (thinc_flags[0] > 0).astype(jnp.float32)
    edge_flags = jnp.broadcast_to(flags[None, :, 0:1, None], (1, planes, 4, lanes))
    edges = jnp.concatenate([own[:, :, 0:2], own[:, :, rows - 2 : rows]], axis=2)
    edges = jnp.concatenate([edges, edge_flags], axis=0)
    halo = lax.ppermute(
        edges, "circ", [(i, (i + 1) % circ_count) for i in range(circ_count)]
    )
    flag_cells = jnp.broadcast_to(flags[:, :, None], (planes, rows, lanes))

    gathered = [
        exchange(jnp.swapaxes(own[first:stop], 0, 1), "inst") for first, stop in CHUNKS
    ]
    res, coup, inv, v, w, coefs = call(
        flux_kernel,
        [
            (planes, FIELDS) + grid,
            (planes,) + grid,
            (planes - 1,) + grid,
            (planes - 1,) + grid,
            (planes - 1,) + grid,
            (COEFS,) + grid,
        ],
        flow_state,
        halo,
        flag_cells,
        flops=own.size * 60,
    )
    gathered, res = lax.optimization_barrier((gathered, res))
    y_parts, sep_parts = [], []
    for (first, stop), block in zip(CHUNKS, gathered):
        fields = stop - first
        (spec,) = call(
            functools.partial(spectral_kernel, weights), [block.shape], block, flops=block.size * 9
        )
        spec = exchange(spec, "inst")
        y, rhs = call(
            functools.partial(sweep_kernel, first),
            [(planes - 1, fields) + grid, (ax_count, 2 * fields + COEFS, piece, lanes)],
            res,
            spec,
            coup,
            inv,
            coefs,
            flops=spec.size * 8,
        )
        rhs = exchange(rhs, "ax")
        (seps,) = call(
            reduced_kernel, [(ax_count, 2 * fields, piece, lanes)], rhs, flops=rhs.size * 8
        )
        sep_parts.append(exchange(seps, "ax"))
        y_parts.append(y)
    (out,) = call(
        functools.partial(finish_kernel, CHUNKS),
        [flow_state.shape],
        flow_state,
        v,
        w,
        *y_parts,
        *sep_parts,
        flops=own.size * 5,
    )
    return out


def solution(mesh):
    return jax.shard_map(
        body,
        mesh=mesh,
        in_specs=(P("inst", None, "ax", "circ", None), P("inst", "ax", "circ")),
        out_specs=P("inst", None, "ax", "circ", None),
        check_vma=False,
    )
```

profile of v0, /device:TPU:1, one launch (start us, length us, event | category | flops | bytes accessed | tf_op | source)
XLA Modules:
  0.0 120.0 jit_solution(12561537423450127627)
XLA Ops:
  0.0 2.9 %copy.9 = f32[1,7,8,64,128]{4,3,1,2,0:T(8,128)} copy(f32[1,7,8,64,128]{4,3,2,1,0:T(8,128)} %state_ref.3) | data formatting | bytes 3670016 | tf_op args[0]
  2.9 0.0 copy-start.3
  2.9 0.0 copy-start
  2.9 6.1 %all-to-all-start = ((f32[8,7,64,128]{3,2,1,0:T(8,128)}), f32[8,7,64,128]{3,2,1,0:T(8,128)}, u32[]{:S(2)}, u32[]{:S(2)}) async-start(f32[8,7,64,128]{3,2,1,0:T(8,128)} %bitcast.8), calls=%async_computation | async-start | bytes 3670016 | tf_op jit(solution)/shard_map/all_to_all | solution.py:294
  9.0 0.0 copy-done.3
  9.0 0.1 slice_reduce_fusion
  9.1 1.1 fusion
  10.2 0.1 broadcast_in_dim.7
  10.3 0.1 pad_maximum_fusion
  10.4 2.5 %collective-permute-start = (f32[8,8,4,128]{3,2,0,1:T(4,128)S(1)}, f32[8,8,4,128]{3,2,0,1:T(4,128)S(1)}, u32[]{:S(2)}, u32[]{:S(2)}) collective-permute-start(f32[8,8,4,128]{3,2,0,1:T(4,128)S(1)} %pad_maximum_fusion), channel_id=1, source_target_pairs={{0,1},{1,0},{2,3},{3,2},{4,5},{5,4},{6,7},{7,6},{8,9},{9,8},{10,11... | collective-permute-start | bytes 393224 | tf_op jit(solution)/shard_map/ppermute | solution.py:311
  12.9 21.7 %collective-permute-done = f32[8,8,4,128]{3,2,0,1:T(4,128)S(1)} collective-permute-done((f32[8,8,4,128]{3,2,0,1:T(4,128)S(1)}, f32[8,8,4,128]{3,2,0,1:T(4,128)S(1)}, u32[]{:S(2)}, u32[]{:S(2)}) %collective-permute-start) | collective-permute-done | bytes 131104 | tf_op jit(solution)/shard_map/ppermute | solution.py:311
  34.6 0.1 broadcast_in_dim.16.flag_ref
  34.8 0.0 copy-done
  34.8 2.5 %shard_map.28 = (f32[8,7,64,128]{3,2,1,0:T(8,128)S(1)}, f32[8,64,128]{2,1,0:T(8,128)S(1)}, f32[7,64,128]{2,1,0:T(8,128)S(1)}, f32[7,64,128]{2,1,0:T(8,128)S(1)},...) custom-call(f32[1,7,8,64,128]{4,3,2,1,0:T(8,128)S(1)} %copy-done, f32[8,8,4,128]{3,2,1,0:T(4,128)S(1)} %copy.6.halo_ref, ...), custom_call_target="tpu_custom_call" | custom-call | flops 27525120 | bytes 5177344 | tf_op jit(solution)/shard_map/pallas_call | solution.py:48
  37.3 0.0 copy-start.1
  37.3 1.2 %copy-done.1 = f32[8,7,64,128]{3,2,1,0:T(8,128)} copy-done((f32[8,7,64,128]{3,2,1,0:T(8,128)}, f32[8,7,64,128]{3,2,1,0:T(8,128)S(1)}, u32[]{:S(2)}) %copy-start.1) | copy-done | bytes 1835032
  38.5 0.0 all-to-all-done.state_ref
  38.5 2.8 %shard_map.29 = f32[8,7,64,128]{3,2,1,0:T(8,128)S(1)} custom-call(f32[8,7,64,128]{3,2,1,0:T(8,128)} %all-to-all-done.state_ref), custom_call_target="tpu_custom_call" | custom-call | flops 4128768 | bytes 3670016 | tf_op jit(solution)/shard_map/pallas_call | solution.py:48
  41.3 0.0 copy-start.2
  41.3 26.2 %all_to_all.20.spec_ref = f32[8,7,64,128]{3,2,1,0:T(8,128)S(1)} all-to-all(f32[8,7,64,128]{3,2,1,0:T(8,128)S(1)} %shard_map.29), channel_id=1, replica_groups=mesh['inst'=8,'ax'=16,'circ'=2] {'inst'}, dimensions={0} | all-to-all | bytes 3670016 | tf_op jit(solution)/shard_map/all_to_all | solution.py:294
  67.6 0.0 copy-done.2
  67.6 0.9 shard_map.30
  68.4 31.1 %all_to_all.21.rhs_ref = f32[16,19,4,128]{3,2,1,0:T(4,128)S(1)} all-to-all(f32[16,19,4,128]{3,2,1,0:T(4,128)S(1)} %get-tuple-element.24), channel_id=1, replica_groups=mesh['inst'=8,'ax'=16,'circ'=2] {'ax'}, dimensions={0} | all-to-all | bytes 1245184 | tf_op jit(solution)/shard_map/all_to_all | solution.py:294
  99.5 0.2 shard_map.31
  99.7 18.4 %all_to_all.22.refs_1_ = f32[16,14,4,128]{3,2,1,0:T(4,128)S(1)} all-to-all(f32[16,14,4,128]{3,2,1,0:T(4,128)S(1)} %shard_map.31), channel_id=1, replica_groups=mesh['inst'=8,'ax'=16,'circ'=2] {'ax'}, dimensions={0} | all-to-all | bytes 917504 | tf_op jit(solution)/shard_map/all_to_all | solution.py:294
  118.1 1.9 %shard_map.32 = f32[1,7,8,64,128]{4,3,2,1,0:T(8,128)} custom-call(f32[1,7,8,64,128]{4,3,2,1,0:T(8,128)S(1)} %copy-done, f32[7,64,128]{2,1,0:T(8,128)S(1)} %get-tuple-element.15.v_ref, f32[7,64,128]{2,1,0:T(8,128)S(1)} %get-tuple-element.16.w_ref, f32[7,7,64,128]{3,2,1,0:T(8,128)S(1)} %get-tuple-element.23.refs_0_, f32[16,14,4,128]{3,2,1,0:T(4,128)S(1)} %all_to_all.22.refs_1_), custom_call_target="tpu_custom_call" | custom-call | flops 2293760 | bytes 6193152 | tf_op jit(solution)/shard_map/pallas_call | solution.py:48
  (2 shorter events, 0.0 us)
Async XLA Ops:
  2.9 6.1 %copy-start.3 = (s32[1,8,64]{2,1,0:T(8,128)S(1)}, s32[1,8,64]{2,1,0:T(8,128)}, u32[]{:S(2)}) copy-start(s32[1,8,64]{2,1,0:T(8,128)} %param.3) | copy-start | bytes 6148
  2.9 31.8 %copy-start = (f32[1,7,8,64,128]{4,3,2,1,0:T(8,128)S(1)}, f32[1,7,8,64,128]{4,3,2,1,0:T(8,128)}, u32[]{:S(2)}) copy-start(f32[1,7,8,64,128]{4,3,2,1,0:T(8,128)} %state_ref.3) | copy-start | bytes 5505028
  2.9 35.6 %all-to-all-start = ((f32[8,7,64,128]{3,2,1,0:T(8,128)}), f32[8,7,64,128]{3,2,1,0:T(8,128)}, u32[]{:S(2)}, u32[]{:S(2)}) async-start(f32[8,7,64,128]{3,2,1,0:T(8,128)} %bitcast.8), calls=%async_computation | async-start | bytes 3670016 | tf_op jit(solution)/shard_map/all_to_all | solution.py:294
  10.4 24.2 %collective-permute-start = (f32[8,8,4,128]{3,2,0,1:T(4,128)S(1)}, f32[8,8,4,128]{3,2,0,1:T(4,128)S(1)}, u32[]{:S(2)}, u32[]{:S(2)}) collective-permute-start(f32[8,8,4,128]{3,2,0,1:T(4,128)S(1)} %pad_maximum_fusion), channel_id=1, source_target_pairs={{0,1},{1,0},{2,3},{3,2},{4,5},{5,4},{6,7},{7,6},{8,9},{9,8},{10,11... | collective-permute-start | bytes 393224 | tf_op jit(solution)/shard_map/ppermute | solution.py:311
  37.3 1.2 %copy-start.1 = (f32[8,7,64,128]{3,2,1,0:T(8,128)}, f32[8,7,64,128]{3,2,1,0:T(8,128)S(1)}, u32[]{:S(2)}) copy-start(f32[8,7,64,128]{3,2,1,0:T(8,128)S(1)} %get-tuple-element.18.res_ref) | copy-start | bytes 5505028
  41.3 26.2 %copy-start.2 = (f32[8,7,64,128]{3,2,1,0:T(8,128)S(1)}, f32[8,7,64,128]{3,2,1,0:T(8,128)}, u32[]{:S(2)}) copy-start(f32[8,7,64,128]{3,2,1,0:T(8,128)} %copy-done.1) | copy-start | bytes 5505028
where the time goes:
time: 120 us
  blocking collectives  75.7 us (63%)
  waiting for transfers between devices  21.7 us (18%)
  starting transfers between devices  8.6 us (7%)
  Pallas kernels  8.29 us (7%)
  local copies, waits for them, and re-layouts  5.6 us (5%)
    all_to_all x3, blocking collectives, exchange(): return lax.all_to_all(x, axis, 0, 0, tiled=True)  75.7 us
    ppermute x1, waiting for transfers between devices, body(): lax.ppermute(edges, 'circ', [(i, (i + 1) % circ_count) for i in range(cir...  21.7 us
    pallas_call x5, Pallas kernels, call(): pl.pallas_call(kernel, out_shape=outs, in_specs=[VMEM] * len(operands), o...  8.29 us
    all_to_all x1, starting transfers between devices, exchange(): return lax.all_to_all(x, axis, 0, 0, tiled=True)  6.07 us
    unnamed x9, local copies, waits for them, and re-layouts  4.18 us
    ppermute x1, starting transfers between devices, body(): lax.ppermute(edges, 'circ', [(i, (i + 1) % circ_count) for i in range(cir...  2.54 us
  transfers between devices with their start and end apart: 2, of which 1 were waited for; matrix products, arithmetic and copies ran while one was open for 1% of the time, Pallas kernels for 2%

commit v1 on v0

--- a/solution.py
+++ b/solution.py
@@ -22,10 +22,10 @@
 FIELDS = 7
 COEFS = 5
 TILE = 8
-CHUNKS = ((0, 7),)
 
 
 VMEM = pl.BlockSpec(memory_space=pltpu.VMEM)
+SMEM = pl.BlockSpec(memory_space=pltpu.SMEM)
 
 
 def spectral_weights(count):
@@ -48,7 +48,7 @@
     return pl.pallas_call(
         kernel,
         out_shape=outs,
-        in_specs=[VMEM] * len(operands),
+        in_specs=[SMEM if x.dtype == jnp.int32 else VMEM for x in operands],
         out_specs=[VMEM] * len(outs),
         compiler_params=pltpu.CompilerParams(vmem_limit_bytes=20 << 20),
         cost_estimate=pl.CostEstimate(flops=flops, bytes_accessed=total, transcendentals=0),
@@ -191,37 +191,69 @@
     lax.fori_loop(0, rows // TILE, factor, 0)
 
 
-def sweep_kernel(first, res_ref, spec_ref, coup_ref, inv_ref, coef_ref, y_ref, red_ref):
+def sweep_kernel(core_ref, res_ref, spec_ref, coup_ref, inv_ref, y_ref, keep_ref, send_ref):
     planes, fields, rows, _ = spec_ref.shape
     last = planes - 1
+    tiles = rows // TILE // 2
+    core = core_ref[0]
+
+    for target_ref, side in ((keep_ref, core), (send_ref, 1 - core)):
+
+        def step(t, _, target_ref=target_ref, side=side):
+            span = pl.ds(pl.multiple_of((side * tiles + t) * TILE, TILE), TILE)
+            place = pl.ds(pl.multiple_of(t * TILE, TILE), TILE)
+            coup = [coup_ref[i, span] for i in range(planes)]
+            inv = [inv_ref[i, span] for i in range(last)]
+            ratio = [coup[i] * inv[i] for i in range(last)]
+            for f in range(fields):
+                value = []
+                for i in range(last):
+                    right = -(res_ref[i, f, span] + spec_ref[i, f, span])
+                    if i:
+                        right = right - coup[i] * value[-1]
+                    value.append(right * inv[i])
+                y = value[-1]
+                y_last = y
+                y_ref[last - 1, f, span] = y
+                for i in range(last - 2, -1, -1):
+                    y = value[i] - ratio[i] * y
+                    y_ref[i, f, span] = y
+                right = -(res_ref[last, f, span] + spec_ref[last, f, span])
+                target_ref[f, place] = y
+                target_ref[fields + f, place] = right - coup[last] * y_last
+            return 0
+
+        lax.fori_loop(0, tiles, step, 0)
+
+
+def merge_kernel(core_ref, keep_ref, got_ref, pair_ref, link_ref, edge_ref, inner_ref, out_ref):
+    fields = inner_ref.shape[0]
+    rows = inner_ref.shape[1]
+    lower_core = core_ref[0] == 0
 
     def step(t, _):
         span = pl.ds(pl.multiple_of(t * TILE, TILE), TILE)
-        coup = [coup_ref[i, span] for i in range(planes)]
-        inv = [inv_ref[i, span] for i in range(last)]
-        ratio = [coup[i] * inv[i] for i in range(last)]
+        inv, sep_a, first_a, lower_b = (pair_ref[k, span] for k in range(4))
+        scale, lower, upper = (link_ref[k, span] for k in range(3))
+        edge = edge_ref[0, span]
         for f in range(fields):
-            value = []
-            for i in range(last):
-                right = -(res_ref[i, first + f, span] + spec_ref[i, f, span])
-                if i:
-                    right = right - coup[i] * value[-1]
-                value.append(right * inv[i])
-            y = value[-1]
-            y_last = y
-            y_ref[last - 1, f, span] = y
-            for i in range(last - 2, -1, -1):
-                y = value[i] - ratio[i] * y
-                y_ref[i, f, span] = y
-            right = -(res_ref[last, first + f, span] + spec_ref[last, f, span])
-            own = right - coup[last] * y_last
-            for k, x in ((f, y), (fields + f, own)):
-                red_ref[2 * t, k] = x[0:4]
-                red_ref[2 * t + 1, k] = x[4:8]
-        for k in range(COEFS):
-            x = coef_ref[k, span]
-            red_ref[2 * t, 2 * fields + k] = x[0:4]
-            red_ref[2 * t + 1, 2 * fields + k] = x[4:8]
+            keep_y, got_y = keep_ref[f, span], got_ref[f, span]
+            keep_own, got_own = keep_ref[fields + f, span], got_ref[fields + f, span]
+            y_a = jnp.where(lower_core, keep_y, got_y)
+            y_b = jnp.where(lower_core, got_y, keep_y)
+            own_a = jnp.where(lower_core, keep_own, got_own)
+            own_b = jnp.where(lower_core, got_own, keep_own)
+            inner = inv * (own_a - sep_a * y_b)
+            inner_ref[f, span] = inner
+            for k, x in (
+                (f, scale * (own_b - lower_b * inner)),
+                (fields + f, edge * (y_a - first_a * inner)),
+            ):
+                out_ref[2 * t, k] = x[0:4]
+                out_ref[2 * t + 1, k] = x[4:8]
+        for k, x in ((2 * fields, lower), (2 * fields + 1, upper)):
+            out_ref[2 * t, k] = x[0:4]
+            out_ref[2 * t + 1, k] = x[4:8]
         return 0
 
     lax.fori_loop(0, rows // TILE, step, 0)
@@ -230,24 +262,18 @@
 def reduced_kernel(rhs_ref, out_ref):
     count = rhs_ref.shape[0]
     fields = out_ref.shape[1] // 2
-    base = 2 * fields
     ratio = []
     values = []
     for p in range(count):
-        lower, diag, sep = rhs_ref[p, base], rhs_ref[p, base + 1], rhs_ref[p, base + 2]
+        lower, upper = rhs_ref[p, 2 * fields], rhs_ref[p, 2 * fields + 1]
         more = p + 1 < count
-        if more:
-            diag = diag - sep * rhs_ref[p + 1, base + 3]
-        if p:
-            diag = diag - lower * ratio[-1]
-        inv = 1.0 / diag
-        if more:
-            ratio.append(-(sep * rhs_ref[p + 1, base + 4]) * inv)
+        inv = 1.0 / (1.0 - lower * ratio[-1]) if p else jnp.ones_like(lower)
+        ratio.append(upper * inv)
         row = []
         for f in range(fields):
-            right = rhs_ref[p, fields + f]
+            right = rhs_ref[p, f]
             if more:
-                right = right - sep * rhs_ref[p + 1, f]
+                right = right - rhs_ref[p + 1, fields + f]
             if p:
                 right = right - lower * values[-1][f]
             row.append(right * inv)
@@ -257,41 +283,61 @@
         if p < count - 1:
             solved = [values[p][f] - ratio[p] * solved[f] for f in range(fields)]
         for f in range(fields):
-            out_ref[p, f] = solved[f]
+            out_ref[p, fields + f] = solved[f]
             if p < count - 1:
-                out_ref[p + 1, fields + f] = solved[f]
+                out_ref[p + 1, f] = solved[f]
     for f in range(fields):
-        out_ref[0, fields + f] = jnp.zeros_like(solved[f])
-
-
-def finish_kernel(chunks, state_ref, v_ref, w_ref, *refs):
-    out_ref = refs[-1]
-    y_refs, sep_refs = refs[: len(chunks)], refs[len(chunks) : 2 * len(chunks)]
-    planes, rows = state_ref.shape[2], state_ref.shape[3]
-    last = planes - 1
+        out_ref[0, f] = jnp.zeros_like(solved[f])
+
+
+def expand_kernel(core_ref, solved_ref, inner_ref, pair_ref, keep_ref, send_ref):
+    fields, rows, _ = inner_ref.shape
+    lower_core = core_ref[0] == 0
 
     def step(t, _):
         span = pl.ds(pl.multiple_of(t * TILE, TILE), TILE)
-        v = [v_ref[i, span] for i in range(last)]
-        w = [w_ref[i, span] for i in range(last)]
-        for (first, stop), y_ref, sep_ref in zip(chunks, y_refs, sep_refs):
-            fields = stop - first
+        v, w = pair_ref[4, span], pair_ref[5, span]
+        for f in range(fields):
+            prev = jnp.concatenate([solved_ref[2 * t, f], solved_ref[2 * t + 1, f]], axis=0)
+            own = jnp.concatenate(
+                [solved_ref[2 * t, fields + f], solved_ref[2 * t + 1, fields + f]], axis=0
+            )
+            inner = inner_ref[f, span] - v * prev - w * own
+            keep_ref[f, span] = jnp.where(lower_core, prev, inner)
+            keep_ref[fields + f, span] = jnp.where(lower_core, inner, own)
+            send_ref[f, span] = jnp.where(lower_core, inner, prev)
+            send_ref[fields + f, span] = jnp.where(lower_core, own, inner)
+        return 0
+
+    lax.fori_loop(0, rows // TILE, step, 0)
+
+
+def finish_kernel(core_ref, state_ref, v_ref, w_ref, y_ref, keep_ref, got_ref, out_ref):
+    fields, planes, rows = state_ref.shape[1:4]
+    last = planes - 1
+    tiles = rows // TILE // 2
+    core = core_ref[0]
+
+    for source_ref, side in ((keep_ref, core), (got_ref, 1 - core)):
+
+        def step(t, _, source_ref=source_ref, side=side):
+            span = pl.ds(pl.multiple_of((side * tiles + t) * TILE, TILE), TILE)
+            place = pl.ds(pl.multiple_of(t * TILE, TILE), TILE)
+            v = [v_ref[i, span] for i in range(last)]
+            w = [w_ref[i, span] for i in range(last)]
             for f in range(fields):
-                own = jnp.concatenate([sep_ref[2 * t, f], sep_ref[2 * t + 1, f]], axis=0)
-                prev = jnp.concatenate(
-                    [sep_ref[2 * t, fields + f], sep_ref[2 * t + 1, fields + f]], axis=0
-                )
+                prev, own = source_ref[f, place], source_ref[fields + f, place]
                 for i in range(last):
                     delta = y_ref[i, f, span] - v[i] * prev - w[i] * own
-                    out_ref[0, first + f, i, span] = state_ref[0, first + f, i, span] + delta
-                out_ref[0, first + f, last, span] = state_ref[0, first + f, last, span] + own
-        return 0
-
-    lax.fori_loop(0, rows // TILE, step, 0)
-
-
-def exchange(x, axis):
-    return lax.all_to_all(x, axis, 0, 0, tiled=True)
+                    out_ref[0, f, i, span] = state_ref[0, f, i, span] + delta
+                out_ref[0, f, last, span] = state_ref[0, f, last, span] + own
+            return 0
+
+        lax.fori_loop(0, tiles, step, 0)
+
+
+def exchange(x, axis, groups=None):
+    return lax.all_to_all(x, axis, 0, 0, tiled=True, axis_index_groups=groups)
 
 
 def body(flow_state, thinc_flags):
@@ -300,9 +346,23 @@
     instances = lax.axis_size("inst")
     ax_count = lax.axis_size("ax")
     circ_count = lax.axis_size("circ")
-    piece = rows // ax_count
+    chips = ax_count // 2
+    half = rows // 2
+    piece = half // chips
     grid = (rows, lanes)
     weights = spectral_weights(instances)
+
+    core = lax.axis_index("ax") % 2
+    core_op = jnp.reshape(core, (1,)).astype(jnp.int32)
+    swap = [(i, i ^ 1) for i in range(ax_count)]
+    groups = [list(range(c, ax_count, 2)) for c in range(2)]
+
+    def partner(x):
+        return lax.ppermute(x, "ax", swap)
+
+    def neighbour(x, by):
+        moves = [(i, i + 2 * by) for i in range(ax_count) if 0 <= i + 2 * by < ax_count]
+        return lax.ppermute(x, "ax", moves)
 
     flags = (thinc_flags[0] > 0).astype(jnp.float32)
     edge_flags = jnp.broadcast_to(flags[None, :, 0:1, None], (1, planes, 4, lanes))
@@ -313,9 +373,13 @@
     )
     flag_cells = jnp.broadcast_to(flags[:, :, None], (planes, rows, lanes))
 
-    gathered = [
-        exchange(jnp.swapaxes(own[first:stop], 0, 1), "inst") for first, stop in CHUNKS
-    ]
+    block = exchange(jnp.swapaxes(own, 0, 1), "inst")
+    block, halo = lax.optimization_barrier((block, halo))
+    (spec,) = call(
+        functools.partial(spectral_kernel, weights), [block.shape], block, flops=block.size * 9
+    )
+    spec = exchange(spec, "inst")
+
     res, coup, inv, v, w, coefs = call(
         flux_kernel,
         [
@@ -331,38 +395,64 @@
         flag_cells,
         flops=own.size * 60,
     )
-    gathered, res = lax.optimization_barrier((gathered, res))
-    y_parts, sep_parts = [], []
-    for (first, stop), block in zip(CHUNKS, gathered):
-        fields = stop - first
-        (spec,) = call(
-            functools.partial(spectral_kernel, weights), [block.shape], block, flops=block.size * 9
-        )
-        spec = exchange(spec, "inst")
-        y, rhs = call(
-            functools.partial(sweep_kernel, first),
-            [(planes - 1, fields) + grid, (ax_count, 2 * fields + COEFS, piece, lanes)],
-            res,
-            spec,
-            coup,
-            inv,
-            coefs,
-            flops=spec.size * 8,
-        )
-        rhs = exchange(rhs, "ax")
-        (seps,) = call(
-            reduced_kernel, [(ax_count, 2 * fields, piece, lanes)], rhs, flops=rhs.size * 8
-        )
-        sep_parts.append(exchange(seps, "ax"))
-        y_parts.append(y)
+    mine = lax.dynamic_slice_in_dim(coefs, core * half, half, axis=1)
+    other = partner(lax.dynamic_slice_in_dim(coefs, (1 - core) * half, half, axis=1))
+    lower_a, diag_a, sep_a, v_a, w_a = jnp.where(core == 0, mine, other)
+    lower_b, diag_b, sep_b, v_b, w_b = jnp.where(core == 0, other, mine)
+    pair_inv = 1.0 / (diag_a - sep_a * v_b)
+    pair_v = pair_inv * lower_a
+    pair_w = -(pair_inv * sep_a * w_b)
+    pair = jnp.stack([pair_inv, sep_a, w_a, lower_b, pair_v, pair_w])
+    ends = neighbour(jnp.stack([v_a - w_a * pair_v, -(w_a * pair_w)]), -1)
+    scale = 1.0 / (diag_b - lower_b * pair_w - sep_b * ends[0])
+    link = jnp.stack([scale, -(lower_b * pair_v) * scale, -(sep_b * ends[1]) * scale])
+    edge = neighbour((sep_b * scale)[None], 1)
+
+    y, keep, send = call(
+        sweep_kernel,
+        [(planes - 1, FIELDS) + grid, (2 * FIELDS, half, lanes), (2 * FIELDS, half, lanes)],
+        core_op,
+        res,
+        spec,
+        coup,
+        inv,
+        flops=spec.size * 8,
+    )
+    inner, rhs = call(
+        merge_kernel,
+        [(FIELDS, half, lanes), (chips, 2 * FIELDS + 2, piece, lanes)],
+        core_op,
+        keep,
+        partner(send),
+        pair,
+        link,
+        edge,
+        flops=send.size * 4,
+    )
+    rhs = exchange(rhs, "ax", groups)
+    (solved,) = call(
+        reduced_kernel, [(chips, 2 * FIELDS, piece, lanes)], rhs, flops=rhs.size * 8
+    )
+    solved = exchange(solved, "ax", groups)
+    keep, send = call(
+        expand_kernel,
+        [(2 * FIELDS, half, lanes)] * 2,
+        core_op,
+        solved,
+        inner,
+        pair,
+        flops=send.size * 4,
+    )
     (out,) = call(
-        functools.partial(finish_kernel, CHUNKS),
+        finish_kernel,
         [flow_state.shape],
+        core_op,
         flow_state,
         v,
         w,
-        *y_parts,
-        *sep_parts,
+        y,
+        keep,
+        partner(send),
         flops=own.size * 5,
     )
     return out

time: 120 us -> 109 us (0.908)
  blocking collectives: 75.7 us -> 30.4 us
  starting transfers between devices: 8.6 us -> 27.3 us
  waiting for transfers between devices: 21.7 us -> 34.2 us
  local copies, waits for them, and re-layouts: 5.6 us -> 8.34 us
    all_to_all x3 -> x2, blocking collectives: 75.7 us -> 30.4 us  [exchange(): return lax.all_to_all(x, axis, 0, 0, tiled=True, axis_index_groups=groups)]
    ppermute x0 -> x5, starting transfers between devices: none -> 14.2 us  [the longest x3 9.38 us: partner(): return lax.ppermute(x, 'ax', swap)]
    ppermute x0 -> x5, waiting for transfers between devices: none -> 7.05 us  [the longest x2 3.95 us: neighbour(): return lax.ppermute(x, 'ax', moves)]
    all_to_all x1 -> x2, waiting for transfers between devices: 0.01 us -> 5.54 us  [exchange(): return lax.all_to_all(x, axis, 0, 0, tiled=True, axis_index_groups=groups)]
    all_to_all x1 -> x2, starting transfers between devices: 6.07 us -> 10.5 us  [exchange(): return lax.all_to_all(x, axis, 0, 0, tiled=True, axis_index_groups=groups)]
    unnamed x9 -> x13, local copies, waits for them, and re-layouts: 4.18 us -> 6.9 us
    pallas_call x5 -> x7, Pallas kernels: 8.29 us -> 8.39 us  [call(): pl.pallas_call(kernel, out_shape=outs, in_specs=[SMEM if x.dtype == jnp.i...]
  transfers between devices with their start and end apart: 2 -> 8, of which waited for: 1 -> 6; matrix products, arithmetic and copies ran while one was open for 1% -> 1% of each run, Pallas kernels for 2% -> 4%
where the time goes in v1:
time: 109 us
  waiting for transfers between devices  34.2 us (31%)
  blocking collectives  30.4 us (28%)
  starting transfers between devices  27.3 us (25%)
  Pallas kernels  8.39 us (8%)
  local copies, waits for them, and re-layouts  8.34 us (8%)
    all_to_all x2, blocking collectives, exchange(): return lax.all_to_all(x, axis, 0, 0, tiled=True, axis_index_groups=groups)  30.4 us
    ppermute x1, waiting for transfers between devices, body(): lax.ppermute(edges, 'circ', [(i, (i + 1) % circ_count) for i in range(cir...  21.6 us
    all_to_all x2, starting transfers between devices, exchange(): return lax.all_to_all(x, axis, 0, 0, tiled=True, axis_index_groups=groups)  10.5 us
    ppermute x3, starting transfers between devices, partner(): return lax.ppermute(x, 'ax', swap)  9.38 us
    pallas_call x7, Pallas kernels, call(): pl.pallas_call(kernel, out_shape=outs, in_specs=[SMEM if x.dtype == jnp.i...  8.39 us
    unnamed x13, local copies, waits for them, and re-layouts  6.9 us
    all_to_all x2, waiting for transfers between devices, exchange(): return lax.all_to_all(x, axis, 0, 0, tiled=True, axis_index_groups=groups)  5.54 us
    ppermute x2, starting transfers between devices, neighbour(): return lax.ppermute(x, 'ax', moves)  4.83 us
  transfers between devices with their start and end apart: 8, of which 6 were waited for; matrix products, arithmetic and copies ran while one was open for 1% of the time, Pallas kernels for 4%

profile of v1, /device:TPU:1, one launch (start us, length us, event | category | flops | bytes accessed | tf_op | source)
XLA Modules:
  0.0 108.9 jit_solution(1295782798190819523)
XLA Ops:
  0.0 2.9 %copy.9 = f32[1,7,8,64,128]{4,3,1,2,0:T(8,128)} copy(f32[1,7,8,64,128]{4,3,2,1,0:T(8,128)} %state_ref.3) | data formatting | bytes 3670016 | tf_op args[0]
  2.9 0.0 copy-start.4
  2.9 6.1 %all-to-all-start = ((f32[8,7,64,128]{3,2,1,0:T(8,128)}), f32[8,7,64,128]{3,2,1,0:T(8,128)S(1)}, u32[]{:S(2)}, u32[]{:S(2)}) async-start(f32[8,7,64,128]{3,2,1,0:T(8,128)} %bitcast.9), calls=%async_computation | async-start | bytes 3670016 | tf_op jit(solution)/shard_map/all_to_all | solution.py:340
  9.0 0.0 copy-done.4
  9.0 0.1 slice_reduce_fusion
  9.1 1.1 %fusion.10 = (f32[7,8,2,128]{3,2,0,1:T(2,128)S(1)}, f32[7,8,2,128]{3,2,0,1:T(2,128)S(1)}) fusion(f32[7,8,64,128]{3,2,0,1:T(8,128)} %bitcast.10), kind=kLoop, calls=%fused_computation.33 | loop fusion | bytes 229376 | tf_op jit(solution)/shard_map/slice | solution.py:369
  10.2 0.1 broadcast_in_dim.7
  10.3 0.1 pad_maximum_fusion
  10.4 2.5 %collective-permute-start = (f32[8,8,4,128]{3,2,0,1:T(4,128)S(1)}, f32[8,8,4,128]{3,2,0,1:T(4,128)S(1)}, u32[]{:S(2)}, u32[]{:S(2)}) collective-permute-start(f32[8,8,4,128]{3,2,0,1:T(4,128)S(1)} %pad_maximum_fusion), channel_id=1, source_target_pairs={{0,1},{1,0},{2,3},{3,2},{4,5},{5,4},{6,7},{7,6},{8,9},{9,8},{10,11... | collective-permute-start | bytes 393224 | tf_op jit(solution)/shard_map/ppermute | solution.py:371
  12.9 21.6 %collective-permute-done = f32[8,8,4,128]{3,2,0,1:T(4,128)S(1)} collective-permute-done((f32[8,8,4,128]{3,2,0,1:T(4,128)S(1)}, f32[8,8,4,128]{3,2,0,1:T(4,128)S(1)}, u32[]{:S(2)}, u32[]{:S(2)}) %collective-permute-start) | collective-permute-done | bytes 131104 | tf_op jit(solution)/shard_map/ppermute | solution.py:371
  34.5 0.0 all-to-all-done.state_ref
  34.5 1.3 %shard_map.29 = f32[8,7,64,128]{3,2,1,0:T(8,128)S(1)} custom-call(f32[8,7,64,128]{3,2,1,0:T(8,128)S(1)} %all-to-all-done.state_ref), custom_call_target="tpu_custom_call" | custom-call | flops 4128768 | bytes 3670016 | tf_op jit(solution)/shard_map/pallas_call | solution.py:48
  35.8 0.0 copy-start.1
  35.8 1.2 %copy-done.1 = f32[8,7,64,128]{3,2,1,0:T(8,128)} copy-done((f32[8,7,64,128]{3,2,1,0:T(8,128)}, f32[8,7,64,128]{3,2,1,0:T(8,128)S(1)}, u32[]{:S(2)}) %copy-start.1) | copy-done | bytes 1835032
  37.1 0.0 copy-start
  37.1 4.5 %all-to-all-start.1 = ((f32[8,7,64,128]{3,2,1,0:T(8,128)}), f32[8,7,64,128]{3,2,1,0:T(8,128)}, u32[]{:S(2)}, u32[]{:S(2)}) async-start(f32[8,7,64,128]{3,2,1,0:T(8,128)} %copy-done.1), calls=%async_computation.1 | async-start | bytes 3670016 | tf_op jit(solution)/shard_map/all_to_all | solution.py:340
  41.6 0.1 broadcast_in_dim.8.flag_ref
  41.7 0.0 copy-done
  41.7 2.5 %shard_map.28 = (f32[8,7,64,128]{3,2,1,0:T(8,128)S(1)}, f32[8,64,128]{2,1,0:T(8,128)S(1)}, f32[7,64,128]{2,1,0:T(8,128)S(1)}, f32[7,64,128]{2,1,0:T(8,128)S(1)},...) custom-call(f32[1,7,8,64,128]{4,3,2,1,0:T(8,128)S(1)} %copy-done, f32[8,8,4,128]{3,2,1,0:T(4,128)S(1)} %copy.6.halo_ref, ...), custom_call_target="tpu_custom_call" | custom-call | flops 27525120 | bytes 5177344 | tf_op jit(solution)/shard_map/pallas_call | solution.py:48
  44.2 0.0 copy-start.2
  44.2 1.2 %copy-done.2 = f32[8,7,64,128]{3,2,1,0:T(8,128)} copy-done((f32[8,7,64,128]{3,2,1,0:T(8,128)}, f32[8,7,64,128]{3,2,1,0:T(8,128)S(1)}, u32[]{:S(2)}) %copy-start.2) | copy-done | bytes 1835032
  45.5 2.4 %collective-permute-start.2 = (f32[5,32,128]{2,1,0:T(8,128)S(1)}, f32[5,32,128]{2,1,0:T(8,128)S(1)}, u32[]{:S(2)}, u32[]{:S(2)}) collective-permute-start(f32[5,32,128]{2,1,0:T(8,128)S(1)} %constant_dynamic-slice_fusion), channel_id=1, source_target_pairs={{0,2},{2,0},{4,6},{6,4},{8,10},{10,8},{12,14},{14,12},{16,18},{18,... | collective-permute-start | bytes 245768 | tf_op jit(solution)/shard_map/ppermute | solution.py:361
  47.8 0.9 collective-permute-done.2
  48.9 1.3 %collective-permute-start.3 = (f32[2,32,128]{2,1,0:T(8,128)S(1)}, f32[2,32,128]{2,1,0:T(8,128)S(1)}, u32[]{:S(2)}, u32[]{:S(2)}) collective-permute-start(f32[2,32,128]{2,1,0:T(8,128)S(1)} %pad_maximum_fusion.2), channel_id=1, source_target_pairs={{4,0},{6,2},{8,4},{10,6},{12,8},{14,10},{16,12},{18,14},{20,16},{2... | collective-permute-start | bytes 98312 | tf_op jit(solution)/shard_map/ppermute | solution.py:365
  50.2 3.9 %collective-permute-done.3 = f32[2,32,128]{2,1,0:T(8,128)S(1)} collective-permute-done((f32[2,32,128]{2,1,0:T(8,128)S(1)}, f32[2,32,128]{2,1,0:T(8,128)S(1)}, u32[]{:S(2)}, u32[]{:S(2)}) %collective-permute-start.3) | collective-permute-done | bytes 32800 | tf_op jit(solution)/shard_map/ppermute | solution.py:365
  54.1 3.5 %collective-permute-start.4 = (f32[1,32,128]{2,1,0:T(8,128)S(1)}, f32[1,32,128]{2,1,0:T(8,128)S(1)}, u32[]{:S(2)}, u32[]{:S(2)}) collective-permute-start(f32[1,32,128]{2,1,0:T(8,128)S(1)} %get-tuple-element.35), channel_id=1, source_target_pairs={{0,4},{2,6},{4,8},{6,10},{8,12},{10,14},{12,16},{14,18},{16,20},{1... | collective-permute-start | bytes 49160 | tf_op jit(solution)/shard_map/ppermute | solution.py:365
  57.7 5.5 %all-to-all-done.1.spec_ref = f32[8,7,64,128]{3,2,1,0:T(8,128)} async-done(((f32[8,7,64,128]{3,2,1,0:T(8,128)}), f32[8,7,64,128]{3,2,1,0:T(8,128)}, u32[]{:S(2)}, u32[]{:S(2)}) %all-to-all-start.1) | async-done | bytes 1835040 | tf_op jit(solution)/shard_map/all_to_all | solution.py:340
  63.2 0.0 copy-start.3
  63.2 1.5 %copy-done.3 = f32[8,7,64,128]{3,2,1,0:T(8,128)S(1)} copy-done((f32[8,7,64,128]{3,2,1,0:T(8,128)S(1)}, f32[8,7,64,128]{3,2,1,0:T(8,128)}, u32[]{:S(2)}) %copy-start.3) | copy-done | bytes 1835032
  64.7 2.4 %shard_map.30 = (f32[7,7,64,128]{3,2,1,0:T(8,128)S(1)}, f32[14,32,128]{2,1,0:T(8,128)S(1)}, f32[14,32,128]{2,1,0:T(8,128)S(1)}) custom-call(s32[1]{0:T(128)} %bitcast.core_ref, f32[8,7,64,128]{3,2,1,0:T(8,128)S(1)} %copy-done.3, f32[8,7,64,128]{3,2,1,0:T(8,128)} %all-to-all-done.1.spec_ref, f32[8,64,128]{2,1,0:T(8,128)S(1)} %get-tuple-element.25.coup_ref, ...), custom_call_target="tpu_custom_call" | custom-call | flops 3670016 | bytes 6225924 | tf_op jit(solution)/shard_map/pallas_call | solution.py:48
  67.1 3.6 %collective-permute-start.1 = (f32[14,32,128]{2,1,0:T(8,128)S(1)}, f32[14,32,128]{2,1,0:T(8,128)S(1)}, u32[]{:S(2)}, u32[]{:S(2)}) collective-permute-start(f32[14,32,128]{2,1,0:T(8,128)S(1)} %get-tuple-element.29), channel_id=1, source_target_pairs={{0,2},{2,0},{4,6},{6,4},{8,10},{10,8},{12,14},{14,12},{16,18},{18,... | collective-permute-start | bytes 688136 | tf_op jit(solution)/shard_map/ppermute | solution.py:361
  70.7 0.0 collective-permute-done.4.edge_ref
  70.7 1.1 collective-permute-done.1.got_ref
  71.8 0.1 shard_map.31
  71.9 19.1 %all_to_all.20.rhs_ref = f32[8,16,4,128]{3,2,1,0:T(4,128)S(1)} all-to-all(f32[8,16,4,128]{3,2,1,0:T(4,128)S(1)} %get-tuple-element.31), channel_id=1, replica_groups={{0,4,8,12,16,20,24,28},{2,6,10,14,18,22,26,30},{1,5,9,13,17,21,25,29},{..., dimensions={0} | all-to-all | bytes 524288 | tf_op jit(solution)/shard_map/all_to_all | solution.py:340
  91.0 0.1 shard_map.32
  91.1 11.3 %all_to_all.21.solved_ref = f32[8,14,4,128]{3,2,1,0:T(4,128)S(1)} all-to-all(f32[8,14,4,128]{3,2,1,0:T(4,128)S(1)} %shard_map.32), channel_id=1, replica_groups={{0,4,8,12,16,20,24,28},{2,6,10,14,18,22,26,30},{1,5,9,13,17,21,25,29},{..., dimensions={0} | all-to-all | bytes 458752 | tf_op jit(solution)/shard_map/all_to_all | solution.py:340
  102.4 0.1 shard_map.33
  102.5 3.4 %collective-permute-start.5 = (f32[14,32,128]{2,1,0:T(8,128)S(1)}, f32[14,32,128]{2,1,0:T(8,128)S(1)}, u32[]{:S(2)}, u32[]{:S(2)}) collective-permute-start(f32[14,32,128]{2,1,0:T(8,128)S(1)} %get-tuple-element.34), channel_id=1, source_target_pairs={{0,2},{2,0},{4,6},{6,4},{8,10},{10,8},{12,14},{14,12},{16,18},{18,... | collective-permute-start | bytes 688136 | tf_op jit(solution)/shard_map/ppermute | solution.py:361
  105.8 1.1 %collective-permute-done.5.got_ref = f32[14,32,128]{2,1,0:T(8,128)S(1)} collective-permute-done((f32[14,32,128]{2,1,0:T(8,128)S(1)}, f32[14,32,128]{2,1,0:T(8,128)S(1)}, u32[]{:S(2)}, u32[]{:S(2)}) %collective-permute-start.5) | collective-permute-done | bytes 229408 | tf_op jit(solution)/shard_map/ppermute | solution.py:361
  107.0 2.0 %shard_map.34 = f32[1,7,8,64,128]{4,3,2,1,0:T(8,128)} custom-call(s32[1]{0:T(128)} %bitcast.core_ref, f32[1,7,8,64,128]{4,3,2,1,0:T(8,128)S(1)} %copy-done, f32[7,64,128]{2,1,0:T(8,128)S(1)} %get-tuple-element.21.v_ref, f32[7,64,128]{2,1,0:T(8,128)S(1)} %get-tuple-element.22.w_ref, f32[7,7,64,128]{3,2,1,0:T(8,128)S(1)} %get-tuple-element.27.y_ref, ...), custom_call_target="tpu_custom_call" | custom-call | flops 2293760 | bytes 6193156 | tf_op jit(solution)/shard_map/pallas_call | solution.py:48
  (13 shorter events, 0.1 us)
Async XLA Ops:
  2.9 6.1 %copy-start.4 = (s32[1,8,64]{2,1,0:T(8,128)S(1)}, s32[1,8,64]{2,1,0:T(8,128)}, u32[]{:S(2)}) copy-start(s32[1,8,64]{2,1,0:T(8,128)} %param.3) | copy-start | bytes 6148
  2.9 31.6 %all-to-all-start = ((f32[8,7,64,128]{3,2,1,0:T(8,128)}), f32[8,7,64,128]{3,2,1,0:T(8,128)S(1)}, u32[]{:S(2)}, u32[]{:S(2)}) async-start(f32[8,7,64,128]{3,2,1,0:T(8,128)} %bitcast.9), calls=%async_computation | async-start | bytes 3670016 | tf_op jit(solution)/shard_map/all_to_all | solution.py:340
  10.4 24.1 %collective-permute-start = (f32[8,8,4,128]{3,2,0,1:T(4,128)S(1)}, f32[8,8,4,128]{3,2,0,1:T(4,128)S(1)}, u32[]{:S(2)}, u32[]{:S(2)}) collective-permute-start(f32[8,8,4,128]{3,2,0,1:T(4,128)S(1)} %pad_maximum_fusion), channel_id=1, source_target_pairs={{0,1},{1,0},{2,3},{3,2},{4,5},{5,4},{6,7},{7,6},{8,9},{9,8},{10,11... | collective-permute-start | bytes 393224 | tf_op jit(solution)/shard_map/ppermute | solution.py:371
  35.8 1.2 %copy-start.1 = (f32[8,7,64,128]{3,2,1,0:T(8,128)}, f32[8,7,64,128]{3,2,1,0:T(8,128)S(1)}, u32[]{:S(2)}) copy-start(f32[8,7,64,128]{3,2,1,0:T(8,128)S(1)} %shard_map.29) | copy-start | bytes 5505028
  37.1 4.6 %copy-start = (f32[1,7,8,64,128]{4,3,2,1,0:T(8,128)S(1)}, f32[1,7,8,64,128]{4,3,2,1,0:T(8,128)}, u32[]{:S(2)}) copy-start(f32[1,7,8,64,128]{4,3,2,1,0:T(8,128)} %state_ref.3) | copy-start | bytes 5505028
  37.1 26.1 %all-to-all-start.1 = ((f32[8,7,64,128]{3,2,1,0:T(8,128)}), f32[8,7,64,128]{3,2,1,0:T(8,128)}, u32[]{:S(2)}, u32[]{:S(2)}) async-start(f32[8,7,64,128]{3,2,1,0:T(8,128)} %copy-done.1), calls=%async_computation.1 | async-start | bytes 3670016 | tf_op jit(solution)/shard_map/all_to_all | solution.py:340
  44.2 1.2 %copy-start.2 = (f32[8,7,64,128]{3,2,1,0:T(8,128)}, f32[8,7,64,128]{3,2,1,0:T(8,128)S(1)}, u32[]{:S(2)}) copy-start(f32[8,7,64,128]{3,2,1,0:T(8,128)S(1)} %get-tuple-element.23.res_ref) | copy-start | bytes 5505028
  45.5 3.3 %collective-permute-start.2 = (f32[5,32,128]{2,1,0:T(8,128)S(1)}, f32[5,32,128]{2,1,0:T(8,128)S(1)}, u32[]{:S(2)}, u32[]{:S(2)}) collective-permute-start(f32[5,32,128]{2,1,0:T(8,128)S(1)} %constant_dynamic-slice_fusion), channel_id=1, source_target_pairs={{0,2},{2,0},{4,6},{6,4},{8,10},{10,8},{12,14},{14,12},{16,18},{18,... | collective-permute-start | bytes 245768 | tf_op jit(solution)/shard_map/ppermute | solution.py:361
  48.9 5.2 %collective-permute-start.3 = (f32[2,32,128]{2,1,0:T(8,128)S(1)}, f32[2,32,128]{2,1,0:T(8,128)S(1)}, u32[]{:S(2)}, u32[]{:S(2)}) collective-permute-start(f32[2,32,128]{2,1,0:T(8,128)S(1)} %pad_maximum_fusion.2), channel_id=1, source_target_pairs={{4,0},{6,2},{8,4},{10,6},{12,8},{14,10},{16,12},{18,14},{20,16},{2... | collective-permute-start | bytes 98312 | tf_op jit(solution)/shard_map/ppermute | solution.py:365
  54.1 16.6 %collective-permute-start.4 = (f32[1,32,128]{2,1,0:T(8,128)S(1)}, f32[1,32,128]{2,1,0:T(8,128)S(1)}, u32[]{:S(2)}, u32[]{:S(2)}) collective-permute-start(f32[1,32,128]{2,1,0:T(8,128)S(1)} %get-tuple-element.35), channel_id=1, source_target_pairs={{0,4},{2,6},{4,8},{6,10},{8,12},{10,14},{12,16},{14,18},{16,20},{1... | collective-permute-start | bytes 49160 | tf_op jit(solution)/shard_map/ppermute | solution.py:365
  63.2 1.5 %copy-start.3 = (f32[8,7,64,128]{3,2,1,0:T(8,128)S(1)}, f32[8,7,64,128]{3,2,1,0:T(8,128)}, u32[]{:S(2)}) copy-start(f32[8,7,64,128]{3,2,1,0:T(8,128)} %copy-done.2) | copy-start | bytes 5505028
  67.1 4.7 %collective-permute-start.1 = (f32[14,32,128]{2,1,0:T(8,128)S(1)}, f32[14,32,128]{2,1,0:T(8,128)S(1)}, u32[]{:S(2)}, u32[]{:S(2)}) collective-permute-start(f32[14,32,128]{2,1,0:T(8,128)S(1)} %get-tuple-element.29), channel_id=1, source_target_pairs={{0,2},{2,0},{4,6},{6,4},{8,10},{10,8},{12,14},{14,12},{16,18},{18,... | collective-permute-start | bytes 688136 | tf_op jit(solution)/shard_map/ppermute | solution.py:361
  102.5 4.5 %collective-permute-start.5 = (f32[14,32,128]{2,1,0:T(8,128)S(1)}, f32[14,32,128]{2,1,0:T(8,128)S(1)}, u32[]{:S(2)}, u32[]{:S(2)}) collective-permute-start(f32[14,32,128]{2,1,0:T(8,128)S(1)} %get-tuple-element.34), channel_id=1, source_target_pairs={{0,2},{2,0},{4,6},{6,4},{8,10},{10,8},{12,14},{14,12},{16,18},{18,... | collective-permute-start | bytes 688136 | tf_op jit(solution)/shard_map/ppermute | solution.py:361

commit v2 on v1

--- a/solution.py
+++ b/solution.py
@@ -25,7 +25,6 @@
 
 
 VMEM = pl.BlockSpec(memory_space=pltpu.VMEM)
-SMEM = pl.BlockSpec(memory_space=pltpu.SMEM)
 
 
 def spectral_weights(count):
@@ -42,41 +41,122 @@
     return table
 
 
-def call(kernel, outs, *operands, flops=0):
+def core_index():
+    return lax.rem(lax.axis_index("ax"), 2)
+
+
+def call(kernel, outs, *operands, flops=0, scratch=()):
     outs = [jax.ShapeDtypeStruct(shape, jnp.float32) for shape in outs]
     total = sum(x.size * 4 for x in operands) + sum(x.size * 4 for x in outs)
-    return pl.pallas_call(
+    run = pl.pallas_call(
         kernel,
         out_shape=outs,
-        in_specs=[SMEM if x.dtype == jnp.int32 else VMEM for x in operands],
+        in_specs=[VMEM] * len(operands),
         out_specs=[VMEM] * len(outs),
-        compiler_params=pltpu.CompilerParams(vmem_limit_bytes=20 << 20),
+        scratch_shapes=[pltpu.VMEM(x, jnp.float32) for x in scratch],
+        compiler_params=pltpu.CompilerParams(
+            vmem_limit_bytes=total + sum(math.prod(x) * 4 for x in scratch) + (2 << 20)
+        ),
         cost_estimate=pl.CostEstimate(flops=flops, bytes_accessed=total, transcendentals=0),
-    )(*operands)
-
-
-def spectral_kernel(weights, state_ref, out_ref):
-    count, fields, rows, _ = state_ref.shape
-    half = count // 2
-    even = [0.5 * (weights[k] + weights[k + half]) for k in range(half)]
-    odd = [0.5 * (weights[k] - weights[k + half]) for k in range(half)]
+    )
+    return list(run(*operands))
+
+
+def slots(count):
+    steps = [(dy, dx) for dy in range(count // 2) for dx in range(2)]
+    return steps
+
+
+def route(dy, dx, count):
+    ring = count // 2
+    return [(i, 2 * ((i // 2 + dy) % ring) + ((i % 2) ^ dx)) for i in range(count)]
+
+
+def pick_kernel(count, state_ref, flag_ref, *refs):
+    outs, edge_ref, sems = refs[:count], refs[count], refs[count + 1]
+    fields, planes, rows = state_ref.shape[1:4]
+    index = lax.axis_index("inst")
+    ring = count // 2
+    places = [
+        2 * lax.rem(index // 2 + dy, ring) + lax.rem(lax.rem(index, 2) + dx, 2)
+        for dy, dx in slots(count)
+    ]
+    copies = [
+        pltpu.make_async_copy(state_ref.at[0, :, place], out, sems.at[k])
+        for k, (place, out) in enumerate(zip(places, outs))
+    ]
+    for copy in copies:
+        copy.start()
+    flags = (flag_ref[0] > 0).astype(jnp.float32)
+    for i in range(planes):
+        edge_ref[i, fields] = jnp.broadcast_to(flags[i : i + 1, 0:1], edge_ref.shape[2:])
+    for copy, place, out in zip(copies, places, outs):
+        copy.wait()
+        for f in range(fields):
+            edge_ref[place, f] = jnp.concatenate(
+                [out[f, 0:2], out[f, rows - 2 : rows]], axis=0
+            )
+
+
+def pick(state, flags, count):
+    _, fields, planes, rows, lanes = state.shape
+    shapes = [(fields, rows, lanes)] * count + [(planes, fields + 1, 4, lanes)]
+    return pl.pallas_call(
+        functools.partial(pick_kernel, count),
+        out_shape=[jax.ShapeDtypeStruct(x, jnp.float32) for x in shapes],
+        in_specs=[pl.BlockSpec(memory_space=pltpu.HBM), VMEM],
+        out_specs=[VMEM] * len(shapes),
+        scratch_shapes=[pltpu.SemaphoreType.DMA((count,))],
+        compiler_params=pltpu.CompilerParams(vmem_limit_bytes=state.size * 4 + (3 << 20)),
+        cost_estimate=pl.CostEstimate(flops=0, bytes_accessed=state.size * 8, transcendentals=0),
+    )(state, flags)
+
+
+def mixing(count, parity):
+    weights = spectral_weights(count)
+    table = []
+    for shift in (0, 1 - 2 * parity, 2 * parity - 1):
+        g = [weights[(2 * a + shift) % count] for a in range(4)]
+        table += [0.5 * (g[0] + g[2]), 0.5 * (g[1] + g[3])]
+        table += [0.5 * (g[0] - g[2]), 0.5 * (g[1] - g[3])]
+    return table
+
+
+def spectral_kernel(*refs):
+    count = len(refs) // 2
+    ins, outs = refs[:count], refs[count:]
+    fields, rows, _ = ins[0].shape
+    tiles = rows // TILE
+    first = lax.rem(lax.axis_index("inst"), 2) == 0
+    mix = [
+        jnp.where(first, jnp.float32(a), jnp.float32(b))
+        for a, b in zip(mixing(count, 0), mixing(count, 1))
+    ]
 
     def step(index, _):
-        field = index // (rows // TILE)
-        span = pl.ds(pl.multiple_of((index % (rows // TILE)) * TILE, TILE), TILE)
-        cells = [state_ref[m, field, span] for m in range(count)]
-        sums = [cells[m] + cells[m + half] for m in range(half)]
-        diffs = [cells[m] - cells[m + half] for m in range(half)]
-        for n in range(half):
-            total = sum(even[(n - m) % half] * sums[m] for m in range(half))
-            alternate = sum(
-                (odd[n - m] if n >= m else -odd[n - m + half]) * diffs[m] for m in range(half)
-            )
-            out_ref[n, field, span] = total + alternate
-            out_ref[n + half, field, span] = total - alternate
+        f = index // tiles
+        span = pl.ds(pl.multiple_of((index % tiles) * TILE, TILE), TILE)
+        parts = []
+        for dx in range(2):
+            u = [ins[2 * dy + dx][f, span] for dy in range(4)]
+            parts.append((u[0] + u[2], u[1] + u[3], u[0] - u[2], u[1] - u[3]))
+        for ex in range(2):
+            even, odd, even_next, odd_next = 0.0, 0.0, 0.0, 0.0
+            for dx in range(2):
+                kind = 0 if ex == dx else (1 if ex else 2)
+                e0, e1, o0, o1 = mix[4 * kind : 4 * kind + 4]
+                s0, s1, d0, d1 = parts[dx]
+                even = even + (e0 * s0 + e1 * s1)
+                odd = odd + (o0 * d0 + o1 * d1)
+                even_next = even_next + (e1 * s0 + e0 * s1)
+                odd_next = odd_next + (o1 * d0 - o0 * d1)
+            outs[ex][f, span] = even + odd
+            outs[4 + ex][f, span] = even - odd
+            outs[2 + ex][f, span] = even_next + odd_next
+            outs[6 + ex][f, span] = even_next - odd_next
         return 0
 
-    lax.fori_loop(0, fields * (rows // TILE), step, 0)
+    lax.fori_loop(0, fields * tiles, step, 0)
 
 
 def primitives(cells):
@@ -102,7 +182,9 @@
     return average + 0.5 * difference * jnp.tanh(BETA * (steepness + offset))
 
 
-def flux_kernel(state_ref, halo_ref, flag_ref, res_ref, coup_ref, inv_ref, v_ref, w_ref, red_ref):
+def flux_kernel(
+    state_ref, halo_ref, flag_ref, res_ref, coup_ref, inv_ref, v_ref, w_ref, keep_ref, send_ref
+):
     planes = state_ref.shape[2]
     rows = state_ref.shape[3]
     last = planes - 1
@@ -110,13 +192,13 @@
     def plane(i, _):
         cells = []
         for f in range(FIELDS):
-            edge = halo_ref[f, i]
+            edge = halo_ref[i, f]
             cells.append(
                 jnp.concatenate(
                     [state_ref[0, f, i], edge[0:2], edge[0:2], edge[2:4], edge[2:4]], axis=0
                 )
             )
-        edge = halo_ref[FIELDS, i]
+        edge = halo_ref[i, FIELDS]
         flags = jnp.concatenate([flag_ref[i], edge, edge], axis=0)
         total = rows + TILE
 
@@ -155,60 +237,102 @@
 
     lax.fori_loop(0, planes, plane, 0)
 
-    def factor(t, _):
-        span = pl.ds(pl.multiple_of(t * TILE, TILE), TILE)
-        coup = [coup_ref[i, span] for i in range(planes)]
-        inv, ratio, v = [], [], []
-        for i in range(last):
-            pivot = DIAG0 - 2.0 * coup[i]
-            if i:
-                pivot = pivot - coup[i] * ratio[-1]
-            inv.append(1.0 / pivot)
-            ratio.append(coup[i] * inv[-1])
-            v.append(inv[-1] if i == 0 else -(ratio[-1] * v[-1]))
-            inv_ref[i, span] = inv[-1]
-        v_next, w_next = v[-1], inv[-1]
-        v_last, w_last = v_next * coup[0], w_next * coup[last - 1]
-        for i in range(last - 1, -1, -1):
-            if i < last - 1:
-                v_next = v[i] - ratio[i] * v_next
-                w_next = -(ratio[i] * w_next)
-            v_first, w_first = v_next * coup[0], w_next * coup[last - 1]
-            v_ref[i, span] = v_first
-            w_ref[i, span] = w_first
-        sep = coup[last]
-        rows_out = (
-            -(sep * v_last),
-            DIAG0 - 2.0 * sep - sep * w_last,
-            sep,
-            v_first,
-            w_first,
-        )
-        for k, value in enumerate(rows_out):
-            red_ref[k, span] = value
-        return 0
-
-    lax.fori_loop(0, rows // TILE, factor, 0)
-
-
-def sweep_kernel(core_ref, res_ref, spec_ref, coup_ref, inv_ref, y_ref, keep_ref, send_ref):
-    planes, fields, rows, _ = spec_ref.shape
+    core = core_index()
+    tiles = rows // TILE // 2
+    for target_ref, side in ((keep_ref, core), (send_ref, 1 - core)):
+
+        def factor(t, _, target_ref=target_ref, side=side):
+            span = pl.ds(pl.multiple_of((side * tiles + t) * TILE, TILE), TILE)
+            place = pl.ds(pl.multiple_of(t * TILE, TILE), TILE)
+            coup = [coup_ref[i, span] for i in range(planes)]
+            inv, ratio, v = [], [], []
+            for i in range(last):
+                pivot = DIAG0 - 2.0 * coup[i]
+                if i:
+                    pivot = pivot - coup[i] * ratio[-1]
+                inv.append(1.0 / pivot)
+                ratio.append(coup[i] * inv[-1])
+                v.append(inv[-1] if i == 0 else -(ratio[-1] * v[-1]))
+                inv_ref[i, span] = inv[-1]
+            v_next, w_next = v[-1], inv[-1]
+            v_last, w_last = v_next * coup[0], w_next * coup[last - 1]
+            for i in range(last - 1, -1, -1):
+                if i < last - 1:
+                    v_next = v[i] - ratio[i] * v_next
+                    w_next = -(ratio[i] * w_next)
+                v_first, w_first = v_next * coup[0], w_next * coup[last - 1]
+                v_ref[i, span] = v_first
+                w_ref[i, span] = w_first
+            sep = coup[last]
+            target_ref[0, place] = -(sep * v_last)
+            target_ref[1, place] = DIAG0 - 2.0 * sep - sep * w_last
+            target_ref[2, place] = sep
+            target_ref[3, place] = v_first
+            target_ref[4, place] = w_first
+            return 0
+
+        lax.fori_loop(0, tiles, factor, 0)
+
+
+def pair_kernel(keep_ref, got_ref, pair_ref, raw_ref, ends_ref):
+    lower_core = core_index() == 0
+    lower_a, diag_a, sep_a, v_a, w_a = (
+        jnp.where(lower_core, keep_ref[k], got_ref[k]) for k in range(COEFS)
+    )
+    lower_b, diag_b, sep_b, v_b, w_b = (
+        jnp.where(lower_core, got_ref[k], keep_ref[k]) for k in range(COEFS)
+    )
+    inv = 1.0 / (diag_a - sep_a * v_b)
+    v = inv * lower_a
+    w = -(inv * sep_a * w_b)
+    for k, x in enumerate((inv, sep_a, w_a, lower_b, v, w)):
+        pair_ref[k] = x
+    raw_ref[0] = diag_b - lower_b * w
+    raw_ref[1] = -(lower_b * v)
+    raw_ref[2] = sep_b
+    ends_ref[0] = v_a - w_a * v
+    ends_ref[1] = -(w_a * w)
+
+
+def link_kernel(raw_ref, ends_ref, link_ref, edge_ref):
+    sep = raw_ref[2]
+    scale = 1.0 / (raw_ref[0] - sep * ends_ref[0])
+    link_ref[0] = scale
+    link_ref[1] = raw_ref[1] * scale
+    link_ref[2] = -(sep * ends_ref[1]) * scale
+    edge_ref[0] = sep * scale
+
+
+def sweep_kernel(res_ref, coup_ref, inv_ref, *refs):
+    count = len(refs) - 4
+    specs = refs[:count]
+    y_ref, keep_ref, send_ref, right_ref = refs[count:]
+    planes, fields, rows, _ = res_ref.shape
     last = planes - 1
     tiles = rows // TILE // 2
-    core = core_ref[0]
+    core = core_index()
+    index = lax.axis_index("inst")
+    ring = count // 2
+    places = [
+        2 * lax.rem(index // 2 + ring - dy, ring) + lax.rem(lax.rem(index, 2) + dx, 2)
+        for dy, dx in slots(count)
+    ]
 
     for target_ref, side in ((keep_ref, core), (send_ref, 1 - core)):
 
         def step(t, _, target_ref=target_ref, side=side):
             span = pl.ds(pl.multiple_of((side * tiles + t) * TILE, TILE), TILE)
             place = pl.ds(pl.multiple_of(t * TILE, TILE), TILE)
+            for f in range(fields):
+                for i, spec_ref in zip(places, specs):
+                    right_ref[f, i] = -(res_ref[i, f, span] + spec_ref[f, span])
             coup = [coup_ref[i, span] for i in range(planes)]
             inv = [inv_ref[i, span] for i in range(last)]
             ratio = [coup[i] * inv[i] for i in range(last)]
             for f in range(fields):
                 value = []
                 for i in range(last):
-                    right = -(res_ref[i, f, span] + spec_ref[i, f, span])
+                    right = right_ref[f, i]
                     if i:
                         right = right - coup[i] * value[-1]
                     value.append(right * inv[i])
@@ -218,18 +342,17 @@
                 for i in range(last - 2, -1, -1):
                     y = value[i] - ratio[i] * y
                     y_ref[i, f, span] = y
-                right = -(res_ref[last, f, span] + spec_ref[last, f, span])
                 target_ref[f, place] = y
-                target_ref[fields + f, place] = right - coup[last] * y_last
+                target_ref[fields + f, place] = right_ref[f, last] - coup[last] * y_last
             return 0
 
         lax.fori_loop(0, tiles, step, 0)
 
 
-def merge_kernel(core_ref, keep_ref, got_ref, pair_ref, link_ref, edge_ref, inner_ref, out_ref):
+def merge_kernel(keep_ref, got_ref, pair_ref, link_ref, edge_ref, inner_ref, out_ref):
     fields = inner_ref.shape[0]
     rows = inner_ref.shape[1]
-    lower_core = core_ref[0] == 0
+    lower_core = core_index() == 0
 
     def step(t, _):
         span = pl.ds(pl.multiple_of(t * TILE, TILE), TILE)
@@ -290,9 +413,9 @@
         out_ref[0, f] = jnp.zeros_like(solved[f])
 
 
-def expand_kernel(core_ref, solved_ref, inner_ref, pair_ref, keep_ref, send_ref):
+def expand_kernel(solved_ref, inner_ref, pair_ref, keep_ref, send_ref):
     fields, rows, _ = inner_ref.shape
-    lower_core = core_ref[0] == 0
+    lower_core = core_index() == 0
 
     def step(t, _):
         span = pl.ds(pl.multiple_of(t * TILE, TILE), TILE)
@@ -312,11 +435,11 @@
     lax.fori_loop(0, rows // TILE, step, 0)
 
 
-def finish_kernel(core_ref, state_ref, v_ref, w_ref, y_ref, keep_ref, got_ref, out_ref):
+def finish_kernel(state_ref, v_ref, w_ref, y_ref, keep_ref, got_ref, out_ref):
     fields, planes, rows = state_ref.shape[1:4]
     last = planes - 1
     tiles = rows // TILE // 2
-    core = core_ref[0]
+    core = core_index()
 
     for source_ref, side in ((keep_ref, core), (got_ref, 1 - core)):
 
@@ -336,6 +459,27 @@
         lax.fori_loop(0, tiles, step, 0)
 
 
+def flux_parts(state, halo, flag_cells):
+    fields, planes, rows, lanes = state.shape[1:]
+    grid = (rows, lanes)
+    return call(
+        flux_kernel,
+        [
+            (planes, fields) + grid,
+            (planes,) + grid,
+            (planes - 1,) + grid,
+            (planes - 1,) + grid,
+            (planes - 1,) + grid,
+            (COEFS, rows // 2, lanes),
+            (COEFS, rows // 2, lanes),
+        ],
+        state,
+        halo,
+        flag_cells,
+        flops=state.size * 60,
+    )
+
+
 def exchange(x, axis, groups=None):
     return lax.all_to_all(x, axis, 0, 0, tiled=True, axis_index_groups=groups)
 
@@ -350,10 +494,7 @@
     half = rows // 2
     piece = half // chips
     grid = (rows, lanes)
-    weights = spectral_weights(instances)
-
-    core = lax.axis_index("ax") % 2
-    core_op = jnp.reshape(core, (1,)).astype(jnp.int32)
+
     swap = [(i, i ^ 1) for i in range(ax_count)]
     groups = [list(range(c, ax_count, 2)) for c in range(2)]
 
@@ -364,64 +505,43 @@
         moves = [(i, i + 2 * by) for i in range(ax_count) if 0 <= i + 2 * by < ax_count]
         return lax.ppermute(x, "ax", moves)
 
-    flags = (thinc_flags[0] > 0).astype(jnp.float32)
-    edge_flags = jnp.broadcast_to(flags[None, :, 0:1, None], (1, planes, 4, lanes))
-    edges = jnp.concatenate([own[:, :, 0:2], own[:, :, rows - 2 : rows]], axis=2)
-    edges = jnp.concatenate([edges, edge_flags], axis=0)
+    steps = slots(instances)
+    blocks = list(pick(flow_state, thinc_flags, instances))
+    edges = blocks.pop()
     halo = lax.ppermute(
         edges, "circ", [(i, (i + 1) % circ_count) for i in range(circ_count)]
     )
+    order = sorted(range(1, instances), key=lambda k: -min(steps[k][0], 4 - steps[k][0]))
+    for k in order:
+        blocks[k] = lax.ppermute(blocks[k], "inst", route(*steps[k], instances))
+    flags = (thinc_flags[0] > 0).astype(jnp.float32)
     flag_cells = jnp.broadcast_to(flags[:, :, None], (planes, rows, lanes))
 
-    block = exchange(jnp.swapaxes(own, 0, 1), "inst")
-    block, halo = lax.optimization_barrier((block, halo))
-    (spec,) = call(
-        functools.partial(spectral_kernel, weights), [block.shape], block, flops=block.size * 9
-    )
-    spec = exchange(spec, "inst")
-
-    res, coup, inv, v, w, coefs = call(
-        flux_kernel,
-        [
-            (planes, FIELDS) + grid,
-            (planes,) + grid,
-            (planes - 1,) + grid,
-            (planes - 1,) + grid,
-            (planes - 1,) + grid,
-            (COEFS,) + grid,
-        ],
-        flow_state,
-        halo,
-        flag_cells,
-        flops=own.size * 60,
-    )
-    mine = lax.dynamic_slice_in_dim(coefs, core * half, half, axis=1)
-    other = partner(lax.dynamic_slice_in_dim(coefs, (1 - core) * half, half, axis=1))
-    lower_a, diag_a, sep_a, v_a, w_a = jnp.where(core == 0, mine, other)
-    lower_b, diag_b, sep_b, v_b, w_b = jnp.where(core == 0, other, mine)
-    pair_inv = 1.0 / (diag_a - sep_a * v_b)
-    pair_v = pair_inv * lower_a
-    pair_w = -(pair_inv * sep_a * w_b)
-    pair = jnp.stack([pair_inv, sep_a, w_a, lower_b, pair_v, pair_w])
-    ends = neighbour(jnp.stack([v_a - w_a * pair_v, -(w_a * pair_w)]), -1)
-    scale = 1.0 / (diag_b - lower_b * pair_w - sep_b * ends[0])
-    link = jnp.stack([scale, -(lower_b * pair_v) * scale, -(sep_b * ends[1]) * scale])
-    edge = neighbour((sep_b * scale)[None], 1)
-
+    res, coup, inv, v, w, keep, send = flux_parts(flow_state, halo, flag_cells)
+
+    thin = (half, lanes)
+    pair, raw, ends = call(
+        pair_kernel, [(6,) + thin, (3,) + thin, (2,) + thin], keep, partner(send)
+    )
+    link, edge = call(link_kernel, [(3,) + thin, (1,) + thin], raw, neighbour(ends, -1))
+    edge = neighbour(edge, 1)
+    blocks, res, link, edge = lax.optimization_barrier((blocks, res, link, edge))
+    specs = call(spectral_kernel, [blocks[0].shape] * instances, *blocks, flops=own.size * 9)
+    for k in order:
+        specs[k] = lax.ppermute(specs[k], "inst", route(*steps[k], instances))
     y, keep, send = call(
         sweep_kernel,
         [(planes - 1, FIELDS) + grid, (2 * FIELDS, half, lanes), (2 * FIELDS, half, lanes)],
-        core_op,
         res,
-        spec,
         coup,
         inv,
-        flops=spec.size * 8,
+        *specs,
+        flops=own.size * 8,
+        scratch=[(FIELDS, planes, TILE, lanes)],
     )
     inner, rhs = call(
         merge_kernel,
         [(FIELDS, half, lanes), (chips, 2 * FIELDS + 2, piece, lanes)],
-        core_op,
         keep,
         partner(send),
         pair,
@@ -437,7 +557,6 @@
     keep, send = call(
         expand_kernel,
         [(2 * FIELDS, half, lanes)] * 2,
-        core_op,
         solved,
         inner,
         pair,
@@ -446,7 +565,6 @@
     (out,) = call(
         finish_kernel,
         [flow_state.shape],
-        core_op,
         flow_state,
         v,
         w,

time: 109 us -> 112 us (1.028)
  starting transfers between devices: 27.3 us -> 45.4 us
  waiting for transfers between devices: 34.2 us -> 25.2 us
  local copies, waits for them, and re-layouts: 8.34 us -> 2.31 us
    ppermute x0 -> x14, starting transfers between devices: none -> 25.5 us  [the longest x7 16.5 us: body(): specs[k] = lax.ppermute(specs[k], 'inst', route(*steps[k], instances))]
    ppermute x0 -> x14, waiting for transfers between devices: none -> 21.3 us  [the longest x7 11.3 us: body(): blocks[k] = lax.ppermute(blocks[k], 'inst', route(*steps[k], instances))]
    ppermute x1, waiting for transfers between devices: 21.6 us -> 0.74 us  [body(): lax.ppermute(edges, 'circ', [(i, (i + 1) % circ_count) for i in range(cir...]
    all_to_all x2 -> x0, starting transfers between devices: 10.5 us -> none  [exchange(): return lax.all_to_all(x, axis, 0, 0, tiled=True, axis_index_groups=groups)]
    all_to_all x2 -> x0, waiting for transfers between devices: 5.54 us -> none  [exchange(): return lax.all_to_all(x, axis, 0, 0, tiled=True, axis_index_groups=groups)]
    unnamed x13 -> x8, local copies, waits for them, and re-layouts: 6.9 us -> 2.19 us
    ppermute x2, waiting for transfers between devices: 3.95 us -> 0.01 us  [neighbour(): return lax.ppermute(x, 'ax', moves)]
    ppermute x3, starting transfers between devices: 9.38 us -> 11.3 us  [partner(): return lax.ppermute(x, 'ax', swap)]
  transfers between devices with their start and end apart: 8 -> 20, of which waited for: 6 -> 9; matrix products, arithmetic and copies ran while one was open for 1% -> 0% of each run, Pallas kernels for 4% -> 2%
where the time goes in v2:
time: 112 us
  starting transfers between devices  45.4 us (41%)
  blocking collectives  31.3 us (28%)
  waiting for transfers between devices  25.2 us (22%)
  Pallas kernels  7.59 us (7%)
  local copies, waits for them, and re-layouts  2.31 us (2%)
    all_to_all x2, blocking collectives, exchange(): return lax.all_to_all(x, axis, 0, 0, tiled=True, axis_index_groups=groups)  31.3 us
    ppermute x7, starting transfers between devices, body(): specs[k] = lax.ppermute(specs[k], 'inst', route(*steps[k], instances))  16.5 us
    ppermute x3, starting transfers between devices, partner(): return lax.ppermute(x, 'ax', swap)  11.3 us
    ppermute x7, waiting for transfers between devices, body(): blocks[k] = lax.ppermute(blocks[k], 'inst', route(*steps[k], instances))  11.3 us
    ppermute x7, waiting for transfers between devices, body(): specs[k] = lax.ppermute(specs[k], 'inst', route(*steps[k], instances))  9.97 us
    ppermute x7, starting transfers between devices, body(): blocks[k] = lax.ppermute(blocks[k], 'inst', route(*steps[k], instances))  8.98 us
    pallas_call x9, Pallas kernels, call(): return list(run(*operands))  7.07 us
    ppermute x2, starting transfers between devices, neighbour(): return lax.ppermute(x, 'ax', moves)  4.95 us
  transfers between devices with their start and end apart: 20, of which 9 were waited for; matrix products, arithmetic and copies ran while one was open for 0% of the time, Pallas kernels for 2%

profile of v2, /device:TPU:1, one launch (start us, length us, event | category | flops | bytes accessed | tf_op | source)
XLA Modules:
  0.0 111.9 jit_solution(9015710660095309706)
XLA Ops:
  0.0 1.5 %copy-done = f32[1,7,8,64,128]{4,3,2,1,0:T(8,128)S(1)} copy-done((f32[1,7,8,64,128]{4,3,2,1,0:T(8,128)S(1)}, f32[1,7,8,64,128]{4,3,2,1,0:T(8,128)}, u32[]{:S(2)}) %copy-start) | copy-done | bytes 1835032
  1.5 0.7 copy-done.2
  2.2 0.5 shard_map.28
  2.7 3.6 %collective-permute-start = (f32[8,8,4,128]{3,2,1,0:T(4,128)S(1)}, f32[8,8,4,128]{3,2,1,0:T(4,128)S(1)}, u32[]{:S(2)}, u32[]{:S(2)}) collective-permute-start(f32[8,8,4,128]{3,2,1,0:T(4,128)S(1)} %get-tuple-element.52), channel_id=1, source_target_pairs={{0,1},{1,0},{2,3},{3,2},{4,5},{5,4},{6,7},{7,6},{8,9},{9,8},{10,11... | collective-permute-start | bytes 393224 | tf_op jit(solution)/shard_map/ppermute | solution.py:511
  6.4 0.3 collective-permute-start.1
  6.7 1.3 %collective-permute-start.2 = (f32[7,64,128]{2,1,0:T(8,128)S(1)}, f32[7,64,128]{2,1,0:T(8,128)S(1)}, u32[]{:S(2)}, u32[]{:S(2)}) collective-permute-start(f32[7,64,128]{2,1,0:T(8,128)S(1)} %get-tuple-element.57), channel_id=1, source_target_pairs={{0,64},{32,96},{64,128},{96,160},{128,192},{160,224},{192,0},{224,... | collective-permute-start | bytes 688136 | tf_op jit(solution)/shard_map/ppermute | solution.py:516
  8.0 0.7 collective-permute-done.halo_ref
  8.7 0.1 broadcast_in_dim.2.flag_ref
  8.9 2.5 %shard_map.29 = (f32[8,7,64,128]{3,2,1,0:T(8,128)S(1)}, f32[8,64,128]{2,1,0:T(8,128)S(1)}, f32[7,64,128]{2,1,0:T(8,128)S(1)}, f32[7,64,128]{2,1,0:T(8,128)S(1)},...) custom-call(f32[1,7,8,64,128]{4,3,2,1,0:T(8,128)S(1)} %copy-done.1, ...), custom_call_target="tpu_custom_call" | custom-call | flops 27525120 | bytes 5177344 | tf_op jit(solution)/shard_map/pallas_call | solution.py:62
  11.4 5.2 %collective-permute-start.8 = (f32[5,32,128]{2,1,0:T(8,128)S(1)}, f32[5,32,128]{2,1,0:T(8,128)S(1)}, u32[]{:S(2)}, u32[]{:S(2)}) collective-permute-start(f32[5,32,128]{2,1,0:T(8,128)S(1)} %get-tuple-element.65), channel_id=1, source_target_pairs={{0,2},{2,0},{4,6},{6,4},{8,10},{10,8},{12,14},{14,12},{16,18},{18,... | collective-permute-start | bytes 245768 | tf_op jit(solution)/shard_map/ppermute | solution.py:502
  16.6 0.9 collective-permute-done.8.got_ref
  17.5 1.3 %collective-permute-start.9 = (f32[2,32,128]{2,1,0:T(8,128)S(1)}, f32[2,32,128]{2,1,0:T(8,128)S(1)}, u32[]{:S(2)}, u32[]{:S(2)}) collective-permute-start(f32[2,32,128]{2,1,0:T(8,128)S(1)} %get-tuple-element.67), channel_id=1, source_target_pairs={{4,0},{6,2},{8,4},{10,6},{12,8},{14,10},{16,12},{18,14},{20,16},{2... | collective-permute-start | bytes 98312 | tf_op jit(solution)/shard_map/ppermute | solution.py:506
  18.8 0.6 collective-permute-start.3
  19.4 2.6 %collective-permute-start.4 = (f32[7,64,128]{2,1,0:T(8,128)S(1)}, f32[7,64,128]{2,1,0:T(8,128)S(1)}, u32[]{:S(2)}, u32[]{:S(2)}) collective-permute-start(f32[7,64,128]{2,1,0:T(8,128)S(1)} %get-tuple-element.59), channel_id=1, source_target_pairs={{0,128},{32,160},{64,192},{96,224},{128,0},{160,32},{192,64},{224,... | collective-permute-start | bytes 688136 | tf_op jit(solution)/shard_map/ppermute | solution.py:516
  22.1 0.2 collective-permute-start.5
  22.2 0.0 collective-permute-done.2.refs_2_
  22.2 3.2 %collective-permute-start.6 = (f32[7,64,128]{2,1,0:T(8,128)S(1)}, f32[7,64,128]{2,1,0:T(8,128)S(1)}, u32[]{:S(2)}, u32[]{:S(2)}) collective-permute-start(f32[7,64,128]{2,1,0:T(8,128)S(1)} %get-tuple-element.61), channel_id=1, source_target_pairs={{0,192},{32,224},{64,0},{96,32},{128,64},{160,96},{192,128},{224,1... | collective-permute-start | bytes 688136 | tf_op jit(solution)/shard_map/ppermute | solution.py:516
  25.5 0.0 collective-permute-done.9.ends_ref
  25.5 0.7 collective-permute-start.7
  26.2 1.7 %collective-permute-done.3.refs_3_ = f32[7,64,128]{2,1,0:T(8,128)S(1)} collective-permute-done((f32[7,64,128]{2,1,0:T(8,128)S(1)}, f32[7,64,128]{2,1,0:T(8,128)S(1)}, u32[]{:S(2)}, u32[]{:S(2)}) %collective-permute-start.3) | collective-permute-done | bytes 229408 | tf_op jit(solution)/shard_map/ppermute | solution.py:516
  27.9 3.7 %collective-permute-start.10 = (f32[1,32,128]{2,1,0:T(8,128)S(1)}, f32[1,32,128]{2,1,0:T(8,128)S(1)}, u32[]{:S(2)}, u32[]{:S(2)}) collective-permute-start(f32[1,32,128]{2,1,0:T(8,128)S(1)} %get-tuple-element.69), channel_id=1, source_target_pairs={{0,4},{2,6},{4,8},{6,10},{8,12},{10,14},{12,16},{14,18},{16,20},{1... | collective-permute-start | bytes 49160 | tf_op jit(solution)/shard_map/ppermute | solution.py:506
  31.6 6.7 %collective-permute-done.4.refs_4_ = f32[7,64,128]{2,1,0:T(8,128)S(1)} collective-permute-done((f32[7,64,128]{2,1,0:T(8,128)S(1)}, f32[7,64,128]{2,1,0:T(8,128)S(1)}, u32[]{:S(2)}, u32[]{:S(2)}) %collective-permute-start.4) | collective-permute-done | bytes 229408 | tf_op jit(solution)/shard_map/ppermute | solution.py:516
  38.3 2.9 %collective-permute-done.6.refs_6_ = f32[7,64,128]{2,1,0:T(8,128)S(1)} collective-permute-done((f32[7,64,128]{2,1,0:T(8,128)S(1)}, f32[7,64,128]{2,1,0:T(8,128)S(1)}, u32[]{:S(2)}, u32[]{:S(2)}) %collective-permute-start.6) | collective-permute-done | bytes 229408 | tf_op jit(solution)/shard_map/ppermute | solution.py:516
  41.2 0.0 collective-permute-done.7.refs_7_
  41.2 0.0 collective-permute-done.10.edge_ref
  41.2 1.3 %shard_map.32 = (f32[7,64,128]{2,1,0:T(8,128)S(1)}, f32[7,64,128]{2,1,0:T(8,128)S(1)}, f32[7,64,128]{2,1,0:T(8,128)S(1)}, f32[7,64,128]{2,1,0:T(8,128)S(1)}, f32...) custom-call(f32[7,64,128]{2,1,0:T(8,128)S(1)} %get-tuple-element.73.r, ...), custom_call_target="tpu_custom_call" | custom-call | flops 4128768 | bytes 3670016 | tf_op jit(solution)/shard_map/pallas_call | solution.py:62
  42.5 2.1 %collective-permute-start.11 = (f32[7,64,128]{2,1,0:T(8,128)S(1)}, f32[7,64,128]{2,1,0:T(8,128)S(1)}, u32[]{:S(2)}, u32[]{:S(2)}) collective-permute-start(f32[7,64,128]{2,1,0:T(8,128)S(1)} %get-tuple-element.82), channel_id=1, source_target_pairs={{0,32},{32,0},{64,96},{96,64},{128,160},{160,128},{192,224},{224,1... | collective-permute-start | bytes 688136 | tf_op jit(solution)/shard_map/ppermute | solution.py:531
  44.6 1.4 %collective-permute-start.12 = (f32[7,64,128]{2,1,0:T(8,128)S(1)}, f32[7,64,128]{2,1,0:T(8,128)S(1)}, u32[]{:S(2)}, u32[]{:S(2)}) collective-permute-start(f32[7,64,128]{2,1,0:T(8,128)S(1)} %get-tuple-element.83), channel_id=1, source_target_pairs={{0,64},{32,96},{64,128},{96,160},{128,192},{160,224},{192,0},{224,... | collective-permute-start | bytes 688136 | tf_op jit(solution)/shard_map/ppermute | solution.py:531
  46.0 1.1 collective-permute-start.13
  47.1 2.0 %collective-permute-start.14 = (f32[7,64,128]{2,1,0:T(8,128)S(1)}, f32[7,64,128]{2,1,0:T(8,128)S(1)}, u32[]{:S(2)}, u32[]{:S(2)}) collective-permute-start(f32[7,64,128]{2,1,0:T(8,128)S(1)} %get-tuple-element.85), channel_id=1, source_target_pairs={{0,128},{32,160},{64,192},{96,224},{128,0},{160,32},{192,64},{224,... | collective-permute-start | bytes 688136 | tf_op jit(solution)/shard_map/ppermute | solution.py:531
  49.1 0.9 collective-permute-start.15
  50.1 0.0 collective-permute-done.11.refs_1_
  50.1 3.4 %collective-permute-start.16 = (f32[7,64,128]{2,1,0:T(8,128)S(1)}, f32[7,64,128]{2,1,0:T(8,128)S(1)}, u32[]{:S(2)}, u32[]{:S(2)}) collective-permute-start(f32[7,64,128]{2,1,0:T(8,128)S(1)} %get-tuple-element.87), channel_id=1, source_target_pairs={{0,192},{32,224},{64,0},{96,32},{128,64},{160,96},{192,128},{224,1... | collective-permute-start | bytes 688136 | tf_op jit(solution)/shard_map/ppermute | solution.py:531
  53.4 3.6 %collective-permute-done.12.refs_2_ = f32[7,64,128]{2,1,0:T(8,128)S(1)} collective-permute-done((f32[7,64,128]{2,1,0:T(8,128)S(1)}, f32[7,64,128]{2,1,0:T(8,128)S(1)}, u32[]{:S(2)}, u32[]{:S(2)}) %collective-permute-start.12) | collective-permute-done | bytes 229408 | tf_op jit(solution)/shard_map/ppermute | solution.py:531
  57.0 5.6 %collective-permute-start.17 = (f32[7,64,128]{2,1,0:T(8,128)S(1)}, f32[7,64,128]{2,1,0:T(8,128)S(1)}, u32[]{:S(2)}, u32[]{:S(2)}) collective-permute-start(f32[7,64,128]{2,1,0:T(8,128)S(1)} %get-tuple-element.88), channel_id=1, source_target_pairs={{0,224},{32,192},{64,32},{96,0},{128,96},{160,64},{192,160},{224,1... | collective-permute-start | bytes 688136 | tf_op jit(solution)/shard_map/ppermute | solution.py:531
  62.6 0.0 collective-permute-done.13.refs_3_
  62.6 6.4 %collective-permute-done.14.refs_4_ = f32[7,64,128]{2,1,0:T(8,128)S(1)} collective-permute-done((f32[7,64,128]{2,1,0:T(8,128)S(1)}, f32[7,64,128]{2,1,0:T(8,128)S(1)}, u32[]{:S(2)}, u32[]{:S(2)}) %collective-permute-start.14) | collective-permute-done | bytes 229408 | tf_op jit(solution)/shard_map/ppermute | solution.py:531
  69.0 1.0 shard_map.33
  70.0 2.7 %collective-permute-start.18 = (f32[14,32,128]{2,1,0:T(8,128)S(1)}, f32[14,32,128]{2,1,0:T(8,128)S(1)}, u32[]{:S(2)}, u32[]{:S(2)}) collective-permute-start(f32[14,32,128]{2,1,0:T(8,128)S(1)} %get-tuple-element.91), channel_id=1, source_target_pairs={{0,2},{2,0},{4,6},{6,4},{8,10},{10,8},{12,14},{14,12},{16,18},{18,... | collective-permute-start | bytes 688136 | tf_op jit(solution)/shard_map/ppermute | solution.py:502
  72.7 1.1 collective-permute-done.18.got_ref
  73.8 0.1 shard_map.34
  74.0 20.0 %all_to_all.10.rhs_ref = f32[8,16,4,128]{3,2,1,0:T(4,128)S(1)} all-to-all(f32[8,16,4,128]{3,2,1,0:T(4,128)S(1)} %get-tuple-element.95), channel_id=1, replica_groups={{0,4,8,12,16,20,24,28},{2,6,10,14,18,22,26,30},{1,5,9,13,17,21,25,29},{..., dimensions={0} | all-to-all | bytes 524288 | tf_op jit(solution)/shard_map/all_to_all | solution.py:484
  93.9 0.1 shard_map.35
  94.0 11.3 %all_to_all.11.solved_ref = f32[8,14,4,128]{3,2,1,0:T(4,128)S(1)} all-to-all(f32[8,14,4,128]{3,2,1,0:T(4,128)S(1)} %shard_map.35), channel_id=1, replica_groups={{0,4,8,12,16,20,24,28},{2,6,10,14,18,22,26,30},{1,5,9,13,17,21,25,29},{..., dimensions={0} | all-to-all | bytes 458752 | tf_op jit(solution)/shard_map/all_to_all | solution.py:484
  105.3 0.1 shard_map.36
  105.4 3.4 %collective-permute-start.19 = (f32[14,32,128]{2,1,0:T(8,128)S(1)}, f32[14,32,128]{2,1,0:T(8,128)S(1)}, u32[]{:S(2)}, u32[]{:S(2)}) collective-permute-start(f32[14,32,128]{2,1,0:T(8,128)S(1)} %get-tuple-element.98), channel_id=1, source_target_pairs={{0,2},{2,0},{4,6},{6,4},{8,10},{10,8},{12,14},{14,12},{16,18},{18,... | collective-permute-start | bytes 688136 | tf_op jit(solution)/shard_map/ppermute | solution.py:502
  108.8 1.1 collective-permute-done.19.got_ref
  109.9 2.0 %shard_map.37 = f32[1,7,8,64,128]{4,3,2,1,0:T(8,128)} custom-call(f32[1,7,8,64,128]{4,3,2,1,0:T(8,128)S(1)} %copy-done.1, f32[7,64,128]{2,1,0:T(8,128)S(1)} %get-tuple-element.53.v_ref, f32[7,64,128]{2,1,0:T(8,128)S(1)} %get-tuple-element.54.w_ref, f32[7,7,64,128]{3,2,1,0:T(8,128)S(1)} %get-tuple-element.89.y_ref, ...), custom_call_target="tpu_custom_call" | custom-call | flops 2293760 | bytes 6193152 | tf_op jit(solution)/shard_map/pallas_call | solution.py:62
  (14 shorter events, 0.1 us)
Async XLA Ops:
  0.0 1.5 %copy-start = (f32[1,7,8,64,128]{4,3,2,1,0:T(8,128)S(1)}, f32[1,7,8,64,128]{4,3,2,1,0:T(8,128)}, u32[]{:S(2)}) copy-start(f32[1,7,8,64,128]{4,3,2,1,0:T(8,128)} %state_ref.5) | copy-start | bytes 5505028
  1.5 0.7 copy-start.2
  2.2 5.8 %copy-start.3 = (s32[1,8,64]{2,1,0:T(8,128)S(1)}, s32[1,8,64]{2,1,0:T(8,128)}, u32[]{:S(2)}) copy-start(s32[1,8,64]{2,1,0:T(8,128)} %flag_ref.1) | copy-start | bytes 6148
  2.2 6.7 %copy-start.1 = (f32[1,7,8,64,128]{4,3,2,1,0:T(8,128)S(1)}, f32[1,7,8,64,128]{4,3,2,1,0:T(8,128)}, u32[]{:S(2)}) copy-start(f32[1,7,8,64,128]{4,3,2,1,0:T(8,128)} %state_ref.5) | copy-start | bytes 5505028
  2.7 6.0 %collective-permute-start = (f32[8,8,4,128]{3,2,1,0:T(4,128)S(1)}, f32[8,8,4,128]{3,2,1,0:T(4,128)S(1)}, u32[]{:S(2)}, u32[]{:S(2)}) collective-permute-start(f32[8,8,4,128]{3,2,1,0:T(4,128)S(1)} %get-tuple-element.52), channel_id=1, source_target_pairs={{0,1},{1,0},{2,3},{3,2},{4,5},{5,4},{6,7},{7,6},{8,9},{9,8},{10,11... | collective-permute-start | bytes 393224 | tf_op jit(solution)/shard_map/ppermute | solution.py:511
  6.4 15.7 %collective-permute-start.1 = (f32[7,64,128]{2,1,0:T(8,128)S(1)}, f32[7,64,128]{2,1,0:T(8,128)S(1)}, u32[]{:S(2)}, u32[]{:S(2)}) collective-permute-start(f32[7,64,128]{2,1,0:T(8,128)S(1)} %get-tuple-element.56), channel_id=1, source_target_pairs={{0,32},{32,0},{64,96},{96,64},{128,160},{160,128},{192,224},{224,1... | collective-permute-start | bytes 688136 | tf_op jit(solution)/shard_map/ppermute | solution.py:516
  6.7 15.6 %collective-permute-start.2 = (f32[7,64,128]{2,1,0:T(8,128)S(1)}, f32[7,64,128]{2,1,0:T(8,128)S(1)}, u32[]{:S(2)}, u32[]{:S(2)}) collective-permute-start(f32[7,64,128]{2,1,0:T(8,128)S(1)} %get-tuple-element.57), channel_id=1, source_target_pairs={{0,64},{32,96},{64,128},{96,160},{128,192},{160,224},{192,0},{224,... | collective-permute-start | bytes 688136 | tf_op jit(solution)/shard_map/ppermute | solution.py:516
  11.4 6.2 %collective-permute-start.8 = (f32[5,32,128]{2,1,0:T(8,128)S(1)}, f32[5,32,128]{2,1,0:T(8,128)S(1)}, u32[]{:S(2)}, u32[]{:S(2)}) collective-permute-start(f32[5,32,128]{2,1,0:T(8,128)S(1)} %get-tuple-element.65), channel_id=1, source_target_pairs={{0,2},{2,0},{4,6},{6,4},{8,10},{10,8},{12,14},{14,12},{16,18},{18,... | collective-permute-start | bytes 245768 | tf_op jit(solution)/shard_map/ppermute | solution.py:502
  17.5 7.9 %collective-permute-start.9 = (f32[2,32,128]{2,1,0:T(8,128)S(1)}, f32[2,32,128]{2,1,0:T(8,128)S(1)}, u32[]{:S(2)}, u32[]{:S(2)}) collective-permute-start(f32[2,32,128]{2,1,0:T(8,128)S(1)} %get-tuple-element.67), channel_id=1, source_target_pairs={{4,0},{6,2},{8,4},{10,6},{12,8},{14,10},{16,12},{18,14},{20,16},{2... | collective-permute-start | bytes 98312 | tf_op jit(solution)/shard_map/ppermute | solution.py:506
  18.8 9.1 %collective-permute-start.3 = (f32[7,64,128]{2,1,0:T(8,128)S(1)}, f32[7,64,128]{2,1,0:T(8,128)S(1)}, u32[]{:S(2)}, u32[]{:S(2)}) collective-permute-start(f32[7,64,128]{2,1,0:T(8,128)S(1)} %get-tuple-element.58), channel_id=1, source_target_pairs={{0,96},{32,64},{64,160},{96,128},{128,224},{160,192},{192,32},{224... | collective-permute-start | bytes 688136 | tf_op jit(solution)/shard_map/ppermute | solution.py:516
  19.4 18.9 %collective-permute-start.4 = (f32[7,64,128]{2,1,0:T(8,128)S(1)}, f32[7,64,128]{2,1,0:T(8,128)S(1)}, u32[]{:S(2)}, u32[]{:S(2)}) collective-permute-start(f32[7,64,128]{2,1,0:T(8,128)S(1)} %get-tuple-element.59), channel_id=1, source_target_pairs={{0,128},{32,160},{64,192},{96,224},{128,0},{160,32},{192,64},{224,... | collective-permute-start | bytes 688136 | tf_op jit(solution)/shard_map/ppermute | solution.py:516
  22.1 16.3 %collective-permute-start.5 = (f32[7,64,128]{2,1,0:T(8,128)S(1)}, f32[7,64,128]{2,1,0:T(8,128)S(1)}, u32[]{:S(2)}, u32[]{:S(2)}) collective-permute-start(f32[7,64,128]{2,1,0:T(8,128)S(1)} %get-tuple-element.60), channel_id=1, source_target_pairs={{0,160},{32,128},{64,224},{96,192},{128,32},{160,0},{192,96},{224,... | collective-permute-start | bytes 688136 | tf_op jit(solution)/shard_map/ppermute | solution.py:516
  22.2 19.0 %collective-permute-start.6 = (f32[7,64,128]{2,1,0:T(8,128)S(1)}, f32[7,64,128]{2,1,0:T(8,128)S(1)}, u32[]{:S(2)}, u32[]{:S(2)}) collective-permute-start(f32[7,64,128]{2,1,0:T(8,128)S(1)} %get-tuple-element.61), channel_id=1, source_target_pairs={{0,192},{32,224},{64,0},{96,32},{128,64},{160,96},{192,128},{224,1... | collective-permute-start | bytes 688136 | tf_op jit(solution)/shard_map/ppermute | solution.py:516
  25.5 15.7 %collective-permute-start.7 = (f32[7,64,128]{2,1,0:T(8,128)S(1)}, f32[7,64,128]{2,1,0:T(8,128)S(1)}, u32[]{:S(2)}, u32[]{:S(2)}) collective-permute-start(f32[7,64,128]{2,1,0:T(8,128)S(1)} %get-tuple-element.62), channel_id=1, source_target_pairs={{0,224},{32,192},{64,32},{96,0},{128,96},{160,64},{192,160},{224,1... | collective-permute-start | bytes 688136 | tf_op jit(solution)/shard_map/ppermute | solution.py:516
  27.9 13.3 %collective-permute-start.10 = (f32[1,32,128]{2,1,0:T(8,128)S(1)}, f32[1,32,128]{2,1,0:T(8,128)S(1)}, u32[]{:S(2)}, u32[]{:S(2)}) collective-permute-start(f32[1,32,128]{2,1,0:T(8,128)S(1)} %get-tuple-element.69), channel_id=1, source_target_pairs={{0,4},{2,6},{4,8},{6,10},{8,12},{10,14},{12,16},{14,18},{16,20},{1... | collective-permute-start | bytes 49160 | tf_op jit(solution)/shard_map/ppermute | solution.py:506
  42.5 7.6 %collective-permute-start.11 = (f32[7,64,128]{2,1,0:T(8,128)S(1)}, f32[7,64,128]{2,1,0:T(8,128)S(1)}, u32[]{:S(2)}, u32[]{:S(2)}) collective-permute-start(f32[7,64,128]{2,1,0:T(8,128)S(1)} %get-tuple-element.82), channel_id=1, source_target_pairs={{0,32},{32,0},{64,96},{96,64},{128,160},{160,128},{192,224},{224,1... | collective-permute-start | bytes 688136 | tf_op jit(solution)/shard_map/ppermute | solution.py:531
  44.6 12.4 %collective-permute-start.12 = (f32[7,64,128]{2,1,0:T(8,128)S(1)}, f32[7,64,128]{2,1,0:T(8,128)S(1)}, u32[]{:S(2)}, u32[]{:S(2)}) collective-permute-start(f32[7,64,128]{2,1,0:T(8,128)S(1)} %get-tuple-element.83), channel_id=1, source_target_pairs={{0,64},{32,96},{64,128},{96,160},{128,192},{160,224},{192,0},{224,... | collective-permute-start | bytes 688136 | tf_op jit(solution)/shard_map/ppermute | solution.py:531
  46.0 16.5 %collective-permute-start.13 = (f32[7,64,128]{2,1,0:T(8,128)S(1)}, f32[7,64,128]{2,1,0:T(8,128)S(1)}, u32[]{:S(2)}, u32[]{:S(2)}) collective-permute-start(f32[7,64,128]{2,1,0:T(8,128)S(1)} %get-tuple-element.84), channel_id=1, source_target_pairs={{0,96},{32,64},{64,160},{96,128},{128,224},{160,192},{192,32},{224... | collective-permute-start | bytes 688136 | tf_op jit(solution)/shard_map/ppermute | solution.py:531
  47.1 21.9 %collective-permute-start.14 = (f32[7,64,128]{2,1,0:T(8,128)S(1)}, f32[7,64,128]{2,1,0:T(8,128)S(1)}, u32[]{:S(2)}, u32[]{:S(2)}) collective-permute-start(f32[7,64,128]{2,1,0:T(8,128)S(1)} %get-tuple-element.85), channel_id=1, source_target_pairs={{0,128},{32,160},{64,192},{96,224},{128,0},{160,32},{192,64},{224,... | collective-permute-start | bytes 688136 | tf_op jit(solution)/shard_map/ppermute | solution.py:531
  49.1 19.8 %collective-permute-start.15 = (f32[7,64,128]{2,1,0:T(8,128)S(1)}, f32[7,64,128]{2,1,0:T(8,128)S(1)}, u32[]{:S(2)}, u32[]{:S(2)}) collective-permute-start(f32[7,64,128]{2,1,0:T(8,128)S(1)} %get-tuple-element.86), channel_id=1, source_target_pairs={{0,160},{32,128},{64,224},{96,192},{128,32},{160,0},{192,96},{224,... | collective-permute-start | bytes 688136 | tf_op jit(solution)/shard_map/ppermute | solution.py:531
  50.1 18.9 %collective-permute-start.16 = (f32[7,64,128]{2,1,0:T(8,128)S(1)}, f32[7,64,128]{2,1,0:T(8,128)S(1)}, u32[]{:S(2)}, u32[]{:S(2)}) collective-permute-start(f32[7,64,128]{2,1,0:T(8,128)S(1)} %get-tuple-element.87), channel_id=1, source_target_pairs={{0,192},{32,224},{64,0},{96,32},{128,64},{160,96},{192,128},{224,1... | collective-permute-start | bytes 688136 | tf_op jit(solution)/shard_map/ppermute | solution.py:531
  57.0 12.0 %collective-permute-start.17 = (f32[7,64,128]{2,1,0:T(8,128)S(1)}, f32[7,64,128]{2,1,0:T(8,128)S(1)}, u32[]{:S(2)}, u32[]{:S(2)}) collective-permute-start(f32[7,64,128]{2,1,0:T(8,128)S(1)} %get-tuple-element.88), channel_id=1, source_target_pairs={{0,224},{32,192},{64,32},{96,0},{128,96},{160,64},{192,160},{224,1... | collective-permute-start | bytes 688136 | tf_op jit(solution)/shard_map/ppermute | solution.py:531
  70.0 3.8 %collective-permute-start.18 = (f32[14,32,128]{2,1,0:T(8,128)S(1)}, f32[14,32,128]{2,1,0:T(8,128)S(1)}, u32[]{:S(2)}, u32[]{:S(2)}) collective-permute-start(f32[14,32,128]{2,1,0:T(8,128)S(1)} %get-tuple-element.91), channel_id=1, source_target_pairs={{0,2},{2,0},{4,6},{6,4},{8,10},{10,8},{12,14},{14,12},{16,18},{18,... | collective-permute-start | bytes 688136 | tf_op jit(solution)/shard_map/ppermute | solution.py:502
  105.4 4.5 %collective-permute-start.19 = (f32[14,32,128]{2,1,0:T(8,128)S(1)}, f32[14,32,128]{2,1,0:T(8,128)S(1)}, u32[]{:S(2)}, u32[]{:S(2)}) collective-permute-start(f32[14,32,128]{2,1,0:T(8,128)S(1)} %get-tuple-element.98), channel_id=1, source_target_pairs={{0,2},{2,0},{4,6},{6,4},{8,10},{10,8},{12,14},{14,12},{16,18},{18,... | collective-permute-start | bytes 688136 | tf_op jit(solution)/shard_map/ppermute | solution.py:502

commit v3 on v2

--- a/solution.py
+++ b/solution.py
@@ -20,6 +20,7 @@
 NU_T = 0.25
 
 FIELDS = 7
+ORDER = (5, 4, 3, 7, 2, 6, 1)
 COEFS = 5
 TILE = 8
 
@@ -73,7 +74,8 @@
 
 
 def pick_kernel(count, state_ref, flag_ref, *refs):
-    outs, edge_ref, sems = refs[:count], refs[count], refs[count + 1]
+    outs = refs[:count]
+    edge_ref, held_ref, sems = refs[count:]
     fields, planes, rows = state_ref.shape[1:4]
     index = lax.axis_index("inst")
     ring = count // 2
@@ -87,7 +89,10 @@
     ]
     for copy in copies:
         copy.start()
-    flags = (flag_ref[0] > 0).astype(jnp.float32)
+    flag_copy = pltpu.make_async_copy(flag_ref, held_ref, sems.at[count])
+    flag_copy.start()
+    flag_copy.wait()
+    flags = (held_ref[0] > 0).astype(jnp.float32)
     for i in range(planes):
         edge_ref[i, fields] = jnp.broadcast_to(flags[i : i + 1, 0:1], edge_ref.shape[2:])
     for copy, place, out in zip(copies, places, outs):
@@ -104,12 +109,15 @@
     return pl.pallas_call(
         functools.partial(pick_kernel, count),
         out_shape=[jax.ShapeDtypeStruct(x, jnp.float32) for x in shapes],
-        in_specs=[pl.BlockSpec(memory_space=pltpu.HBM), VMEM],
+        in_specs=[pl.BlockSpec(memory_space=pltpu.HBM)] * 2,
         out_specs=[VMEM] * len(shapes),
-        scratch_shapes=[pltpu.SemaphoreType.DMA((count,))],
+        scratch_shapes=[
+            pltpu.VMEM(flags.shape, flags.dtype),
+            pltpu.SemaphoreType.DMA((count + 1,)),
+        ],
         compiler_params=pltpu.CompilerParams(vmem_limit_bytes=state.size * 4 + (3 << 20)),
         cost_estimate=pl.CostEstimate(flops=0, bytes_accessed=state.size * 8, transcendentals=0),
-    )(state, flags)
+    )(*(pltpu.with_memory_space_constraint(x, pltpu.HBM) for x in (state, flags)))
 
 
 def mixing(count, parity):
@@ -303,14 +311,19 @@
     edge_ref[0] = sep * scale
 
 
-def sweep_kernel(res_ref, coup_ref, inv_ref, *refs):
-    count = len(refs) - 4
+def half_of(mine):
+    core = core_index()
+    return core if mine else 1 - core
+
+
+def sweep_kernel(mine, res_ref, coup_ref, inv_ref, *refs):
+    count = len(refs) - 3
     specs = refs[:count]
-    y_ref, keep_ref, send_ref, right_ref = refs[count:]
+    y_ref, target_ref, right_ref = refs[count:]
     planes, fields, rows, _ = res_ref.shape
     last = planes - 1
     tiles = rows // TILE // 2
-    core = core_index()
+    side = half_of(mine)
     index = lax.axis_index("inst")
     ring = count // 2
     places = [
@@ -318,35 +331,33 @@
         for dy, dx in slots(count)
     ]
 
-    for target_ref, side in ((keep_ref, core), (send_ref, 1 - core)):
-
-        def step(t, _, target_ref=target_ref, side=side):
-            span = pl.ds(pl.multiple_of((side * tiles + t) * TILE, TILE), TILE)
-            place = pl.ds(pl.multiple_of(t * TILE, TILE), TILE)
-            for f in range(fields):
-                for i, spec_ref in zip(places, specs):
-                    right_ref[f, i] = -(res_ref[i, f, span] + spec_ref[f, span])
-            coup = [coup_ref[i, span] for i in range(planes)]
-            inv = [inv_ref[i, span] for i in range(last)]
-            ratio = [coup[i] * inv[i] for i in range(last)]
-            for f in range(fields):
-                value = []
-                for i in range(last):
-                    right = right_ref[f, i]
-                    if i:
-                        right = right - coup[i] * value[-1]
-                    value.append(right * inv[i])
-                y = value[-1]
-                y_last = y
-                y_ref[last - 1, f, span] = y
-                for i in range(last - 2, -1, -1):
-                    y = value[i] - ratio[i] * y
-                    y_ref[i, f, span] = y
-                target_ref[f, place] = y
-                target_ref[fields + f, place] = right_ref[f, last] - coup[last] * y_last
-            return 0
-
-        lax.fori_loop(0, tiles, step, 0)
+    def step(t, _):
+        span = pl.ds(pl.multiple_of((side * tiles + t) * TILE, TILE), TILE)
+        place = pl.ds(pl.multiple_of(t * TILE, TILE), TILE)
+        for f in range(fields):
+            for i, spec_ref in zip(places, specs):
+                right_ref[f, i] = -(res_ref[i, f, span] + spec_ref[f, span])
+        coup = [coup_ref[i, span] for i in range(planes)]
+        inv = [inv_ref[i, span] for i in range(last)]
+        ratio = [coup[i] * inv[i] for i in range(last)]
+        for f in range(fields):
+            value = []
+            for i in range(last):
+                right = right_ref[f, i]
+                if i:
+                    right = right - coup[i] * value[-1]
+                value.append(right * inv[i])
+            y = value[-1]
+            y_last = y
+            y_ref[last - 1, f, place] = y
+            for i in range(last - 2, -1, -1):
+                y = value[i] - ratio[i] * y
+                y_ref[i, f, place] = y
+            target_ref[f, place] = y
+            target_ref[fields + f, place] = right_ref[f, last] - coup[last] * y_last
+        return 0
+
+    lax.fori_loop(0, tiles, step, 0)
 
 
 def merge_kernel(keep_ref, got_ref, pair_ref, link_ref, edge_ref, inner_ref, out_ref):
@@ -435,28 +446,61 @@
     lax.fori_loop(0, rows // TILE, step, 0)
 
 
-def finish_kernel(state_ref, v_ref, w_ref, y_ref, keep_ref, got_ref, out_ref):
+def finish_kernel(mine, state_ref, v_ref, w_ref, y_ref, ends_ref, *refs):
+    out_ref, block_ref, sems = refs[-3:]
     fields, planes, rows = state_ref.shape[1:4]
     last = planes - 1
     tiles = rows // TILE // 2
-    core = core_index()
-
-    for source_ref, side in ((keep_ref, core), (got_ref, 1 - core)):
-
-        def step(t, _, source_ref=source_ref, side=side):
-            span = pl.ds(pl.multiple_of((side * tiles + t) * TILE, TILE), TILE)
-            place = pl.ds(pl.multiple_of(t * TILE, TILE), TILE)
-            v = [v_ref[i, span] for i in range(last)]
-            w = [w_ref[i, span] for i in range(last)]
-            for f in range(fields):
-                prev, own = source_ref[f, place], source_ref[fields + f, place]
-                for i in range(last):
-                    delta = y_ref[i, f, span] - v[i] * prev - w[i] * own
-                    out_ref[0, f, i, span] = state_ref[0, f, i, span] + delta
-                out_ref[0, f, last, span] = state_ref[0, f, last, span] + own
+    side = half_of(mine)
+    copies = []
+    for t in range(tiles):
+        span = pl.ds(pl.multiple_of((side * tiles + t) * TILE, TILE), TILE)
+        place = pl.ds(t * TILE, TILE)
+
+        def field(f, _, span=span, place=place, t=t):
+            prev, own = ends_ref[f, place], ends_ref[fields + f, place]
+            for i in range(last):
+                delta = y_ref[i, f, place] - v_ref[i, span] * prev - w_ref[i, span] * own
+                block_ref[t, f, i] = state_ref[0, f, i, span] + delta
+            block_ref[t, f, last] = state_ref[0, f, last, span] + own
             return 0
 
-        lax.fori_loop(0, tiles, step, 0)
+        lax.fori_loop(0, fields, field, 0)
+        copy = pltpu.make_async_copy(
+            block_ref.at[t], out_ref.at[0, :, :, span], sems.at[t]
+        )
+        copy.start()
+        copies.append(copy)
+    for copy in copies:
+        copy.wait()
+
+
+def finish(mine, state, v, w, y, ends, partial=None):
+    fields, planes, rows, lanes = state.shape[1:]
+    tiles = rows // TILE // 2
+    hbm = pl.BlockSpec(memory_space=pltpu.HBM)
+    operands = [state, v, w, y, ends]
+    specs = [VMEM] * len(operands)
+    aliases = {}
+    if partial is not None:
+        aliases = {len(operands): 0}
+        operands.append(partial)
+        specs.append(hbm)
+    return pl.pallas_call(
+        functools.partial(finish_kernel, mine),
+        out_shape=jax.ShapeDtypeStruct(state.shape, jnp.float32),
+        in_specs=specs,
+        out_specs=hbm,
+        scratch_shapes=[
+            pltpu.VMEM((tiles, fields, planes, TILE, lanes), jnp.float32),
+            pltpu.SemaphoreType.DMA((tiles,)),
+        ],
+        input_output_aliases=aliases,
+        compiler_params=pltpu.CompilerParams(vmem_limit_bytes=state.size * 12),
+        cost_estimate=pl.CostEstimate(
+            flops=state.size * 2, bytes_accessed=state.size * 6, transcendentals=0
+        ),
+    )(*operands)
 
 
 def flux_parts(state, halo, flag_cells):
@@ -493,7 +537,6 @@
     chips = ax_count // 2
     half = rows // 2
     piece = half // chips
-    grid = (rows, lanes)
 
     swap = [(i, i ^ 1) for i in range(ax_count)]
     groups = [list(range(c, ax_count, 2)) for c in range(2)]
@@ -511,7 +554,7 @@
     halo = lax.ppermute(
         edges, "circ", [(i, (i + 1) % circ_count) for i in range(circ_count)]
     )
-    order = sorted(range(1, instances), key=lambda k: -min(steps[k][0], 4 - steps[k][0]))
+    order = ORDER
     for k in order:
         blocks[k] = lax.ppermute(blocks[k], "inst", route(*steps[k], instances))
     flags = (thinc_flags[0] > 0).astype(jnp.float32)
@@ -523,22 +566,29 @@
     pair, raw, ends = call(
         pair_kernel, [(6,) + thin, (3,) + thin, (2,) + thin], keep, partner(send)
     )
-    link, edge = call(link_kernel, [(3,) + thin, (1,) + thin], raw, neighbour(ends, -1))
-    edge = neighbour(edge, 1)
-    blocks, res, link, edge = lax.optimization_barrier((blocks, res, link, edge))
+    blocks, res, ends = lax.optimization_barrier((blocks, res, ends))
     specs = call(spectral_kernel, [blocks[0].shape] * instances, *blocks, flops=own.size * 9)
     for k in order:
         specs[k] = lax.ppermute(specs[k], "inst", route(*steps[k], instances))
-    y, keep, send = call(
-        sweep_kernel,
-        [(planes - 1, FIELDS) + grid, (2 * FIELDS, half, lanes), (2 * FIELDS, half, lanes)],
-        res,
-        coup,
-        inv,
-        *specs,
-        flops=own.size * 8,
-        scratch=[(FIELDS, planes, TILE, lanes)],
-    )
+    ends = neighbour(ends, -1)
+    link, edge = call(link_kernel, [(3,) + thin, (1,) + thin], raw, ends)
+    edge = neighbour(edge, 1)
+    shapes = [(planes - 1, FIELDS, half, lanes), (2 * FIELDS, half, lanes)]
+    parts = []
+    for mine in (False, True):
+        parts.append(
+            call(
+                functools.partial(sweep_kernel, mine),
+                shapes,
+                res,
+                coup,
+                inv,
+                *specs,
+                flops=own.size * 4,
+                scratch=[(FIELDS, planes, TILE, lanes)],
+            )
+        )
+    (y_other, send), (y_mine, keep) = parts
     inner, rhs = call(
         merge_kernel,
         [(FIELDS, half, lanes), (chips, 2 * FIELDS + 2, piece, lanes)],
@@ -562,18 +612,9 @@
         pair,
         flops=send.size * 4,
     )
-    (out,) = call(
-        finish_kernel,
-        [flow_state.shape],
-        flow_state,
-        v,
-        w,
-        y,
-        keep,
-        partner(send),
-        flops=own.size * 5,
-    )
-    return out
+    got = partner(send)
+    out = finish(True, flow_state, v, w, y_mine, keep)
+    return finish(False, flow_state, v, w, y_other, got, out)
 
 
 def solution(mesh):

time: 112 us -> 116 us (1.036)
  starting transfers between devices: 45.4 us -> 50 us
  local copies, waits for them, and re-layouts: 2.31 us -> 0.13 us
  Pallas kernels: 7.59 us -> 9.44 us
  blocking collectives: 31.3 us -> 29.5 us
  waiting for transfers between devices: 25.2 us -> 26.6 us
    ppermute x2, waiting for transfers between devices: 0.01 us -> 4.2 us  [neighbour(): return lax.ppermute(x, 'ax', moves)]
    ppermute x7, waiting for transfers between devices: 11.3 us -> 15.2 us  [body(): blocks[k] = lax.ppermute(blocks[k], 'inst', route(*steps[k], instances))]
    ppermute x7, waiting for transfers between devices: 9.97 us -> 6.42 us  [body(): specs[k] = lax.ppermute(specs[k], 'inst', route(*steps[k], instances))]
    ppermute x7, starting transfers between devices: 16.5 us -> 19.7 us  [body(): specs[k] = lax.ppermute(specs[k], 'inst', route(*steps[k], instances))]
    ppermute x3, waiting for transfers between devices: 3.15 us -> 0.01 us  [partner(): return lax.ppermute(x, 'ax', swap)]
    pallas_call x0 -> x2, Pallas kernels: none -> 2.53 us  [finish(): pl.pallas_call(functools.partial(finish_kernel, mine), out_shape=jax.Shap...]
    unnamed x8 -> x4, local copies, waits for them, and re-layouts: 2.19 us -> 0.01 us
    pallas_call x9, Pallas kernels: 7.07 us -> 5.14 us  [call(): return list(run(*operands))]
  transfers between devices with their start and end apart: 20 -> 20, of which waited for: 9 -> 7; matrix products, arithmetic and copies ran while one was open for 0% -> 0% of each run, Pallas kernels for 2% -> 4%
where the time goes in v3:
time: 116 us
  starting transfers between devices  50 us (43%)
  blocking collectives  29.5 us (25%)
  waiting for transfers between devices  26.6 us (23%)
  Pallas kernels  9.44 us (8%)
    all_to_all x2, blocking collectives, exchange(): return lax.all_to_all(x, axis, 0, 0, tiled=True, axis_index_groups=groups)  29.5 us
    ppermute x7, starting transfers between devices, body(): specs[k] = lax.ppermute(specs[k], 'inst', route(*steps[k], instances))  19.7 us
    ppermute x7, waiting for transfers between devices, body(): blocks[k] = lax.ppermute(blocks[k], 'inst', route(*steps[k], instances))  15.2 us
    ppermute x3, starting transfers between devices, partner(): return lax.ppermute(x, 'ax', swap)  13 us
    ppermute x7, starting transfers between devices, body(): blocks[k] = lax.ppermute(blocks[k], 'inst', route(*steps[k], instances))  8.9 us
    ppermute x7, waiting for transfers between devices, body(): specs[k] = lax.ppermute(specs[k], 'inst', route(*steps[k], instances))  6.42 us
    pallas_call x9, Pallas kernels, call(): return list(run(*operands))  5.14 us
    ppermute x2, starting transfers between devices, neighbour(): return lax.ppermute(x, 'ax', moves)  4.82 us
  transfers between devices with their start and end apart: 20, of which 7 were waited for; matrix products, arithmetic and copies ran while one was open for 0% of the time, Pallas kernels for 4%

profile of v3, /device:TPU:1, one launch (start us, length us, event | category | flops | bytes accessed | tf_op | source)
XLA Modules:
  0.0 115.9 jit_solution(9289818181941256787)
XLA Ops:
  0.0 1.8 %shard_map.28 = (f32[7,64,128]{2,1,0:T(8,128)S(1)}, f32[7,64,128]{2,1,0:T(8,128)S(1)}, f32[7,64,128]{2,1,0:T(8,128)S(1)}, f32[7,64,128]{2,1,0:T(8,128)S(1)}, f32...) custom-call(f32[1,7,8,64,128]{4,3,2,1,0:T(8,128)} %state_ref.7, ...), custom_call_target="tpu_custom_call" | custom-call | bytes 3670016 | tf_op jit(solution)/shard_map/pallas_call | solution.py:109
  1.8 3.6 %collective-permute-start = (f32[8,8,4,128]{3,2,1,0:T(4,128)S(1)}, f32[8,8,4,128]{3,2,1,0:T(4,128)S(1)}, u32[]{:S(2)}, u32[]{:S(2)}) collective-permute-start(f32[8,8,4,128]{3,2,1,0:T(4,128)S(1)} %get-tuple-element.52), channel_id=1, source_target_pairs={{0,1},{1,0},{2,3},{3,2},{4,5},{5,4},{6,7},{7,6},{8,9},{9,8},{10,11... | collective-permute-start | bytes 393224 | tf_op jit(solution)/shard_map/ppermute | solution.py:554
  5.4 0.3 collective-permute-start.1
  5.8 1.3 %collective-permute-start.2 = (f32[7,64,128]{2,1,0:T(8,128)S(1)}, f32[7,64,128]{2,1,0:T(8,128)S(1)}, u32[]{:S(2)}, u32[]{:S(2)}) collective-permute-start(f32[7,64,128]{2,1,0:T(8,128)S(1)} %get-tuple-element.57), channel_id=1, source_target_pairs={{0,64},{32,96},{64,128},{96,160},{128,192},{160,224},{192,0},{224,... | collective-permute-start | bytes 688136 | tf_op jit(solution)/shard_map/ppermute | solution.py:559
  7.1 0.7 collective-permute-done.halo_ref
  7.8 0.1 broadcast_in_dim.2.flag_ref
  7.9 2.5 %shard_map.29 = (f32[8,7,64,128]{3,2,1,0:T(8,128)S(1)}, f32[8,64,128]{2,1,0:T(8,128)S(1)}, f32[7,64,128]{2,1,0:T(8,128)S(1)}, f32[7,64,128]{2,1,0:T(8,128)S(1)},...) custom-call(f32[1,7,8,64,128]{4,3,2,1,0:T(8,128)S(1)} %copy-done, ...), custom_call_target="tpu_custom_call" | custom-call | flops 27525120 | bytes 5177344 | tf_op jit(solution)/shard_map/pallas_call | solution.py:63
  10.4 5.2 %collective-permute-start.8 = (f32[5,32,128]{2,1,0:T(8,128)S(1)}, f32[5,32,128]{2,1,0:T(8,128)S(1)}, u32[]{:S(2)}, u32[]{:S(2)}) collective-permute-start(f32[5,32,128]{2,1,0:T(8,128)S(1)} %get-tuple-element.65), channel_id=1, source_target_pairs={{0,2},{2,0},{4,6},{6,4},{8,10},{10,8},{12,14},{14,12},{16,18},{18,... | collective-permute-start | bytes 245768 | tf_op jit(solution)/shard_map/ppermute | solution.py:545
  15.7 0.5 collective-permute-start.3
  16.2 2.6 %collective-permute-start.4 = (f32[7,64,128]{2,1,0:T(8,128)S(1)}, f32[7,64,128]{2,1,0:T(8,128)S(1)}, u32[]{:S(2)}, u32[]{:S(2)}) collective-permute-start(f32[7,64,128]{2,1,0:T(8,128)S(1)} %get-tuple-element.59), channel_id=1, source_target_pairs={{0,128},{32,160},{64,192},{96,224},{128,0},{160,32},{192,64},{224,... | collective-permute-start | bytes 688136 | tf_op jit(solution)/shard_map/ppermute | solution.py:559
  18.8 0.0 collective-permute-done.8.got_ref
  18.8 0.2 collective-permute-start.5
  19.0 0.0 collective-permute-done.1.refs_1_
  19.0 3.2 %collective-permute-start.6 = (f32[7,64,128]{2,1,0:T(8,128)S(1)}, f32[7,64,128]{2,1,0:T(8,128)S(1)}, u32[]{:S(2)}, u32[]{:S(2)}) collective-permute-start(f32[7,64,128]{2,1,0:T(8,128)S(1)} %get-tuple-element.61), channel_id=1, source_target_pairs={{0,192},{32,224},{64,0},{96,32},{128,64},{160,96},{192,128},{224,1... | collective-permute-start | bytes 688136 | tf_op jit(solution)/shard_map/ppermute | solution.py:559
  22.2 0.0 collective-permute-done.2.refs_2_
  22.2 0.7 collective-permute-start.7
  23.0 1.9 %collective-permute-done.3.refs_3_ = f32[7,64,128]{2,1,0:T(8,128)S(1)} collective-permute-done((f32[7,64,128]{2,1,0:T(8,128)S(1)}, f32[7,64,128]{2,1,0:T(8,128)S(1)}, u32[]{:S(2)}, u32[]{:S(2)}) %collective-permute-start.3) | collective-permute-done | bytes 229408 | tf_op jit(solution)/shard_map/ppermute | solution.py:559
  24.9 10.2 %collective-permute-done.4.refs_4_ = f32[7,64,128]{2,1,0:T(8,128)S(1)} collective-permute-done((f32[7,64,128]{2,1,0:T(8,128)S(1)}, f32[7,64,128]{2,1,0:T(8,128)S(1)}, u32[]{:S(2)}, u32[]{:S(2)}) %collective-permute-start.4) | collective-permute-done | bytes 229408 | tf_op jit(solution)/shard_map/ppermute | solution.py:559
  35.1 0.0 collective-permute-done.5.refs_5_
  35.1 3.1 %collective-permute-done.6.refs_6_ = f32[7,64,128]{2,1,0:T(8,128)S(1)} collective-permute-done((f32[7,64,128]{2,1,0:T(8,128)S(1)}, f32[7,64,128]{2,1,0:T(8,128)S(1)}, u32[]{:S(2)}, u32[]{:S(2)}) %collective-permute-start.6) | collective-permute-done | bytes 229408 | tf_op jit(solution)/shard_map/ppermute | solution.py:559
  38.2 0.0 collective-permute-done.7.refs_7_
  38.2 1.3 %shard_map.31 = (f32[7,64,128]{2,1,0:T(8,128)S(1)}, f32[7,64,128]{2,1,0:T(8,128)S(1)}, f32[7,64,128]{2,1,0:T(8,128)S(1)}, f32[7,64,128]{2,1,0:T(8,128)S(1)}, f32...) custom-call(f32[7,64,128]{2,1,0:T(8,128)S(1)} %get-tuple-element.70.r, ...), custom_call_target="tpu_custom_call" | custom-call | flops 4128768 | bytes 3670016 | tf_op jit(solution)/shard_map/pallas_call | solution.py:63
  39.5 2.1 %collective-permute-start.9 = (f32[7,64,128]{2,1,0:T(8,128)S(1)}, f32[7,64,128]{2,1,0:T(8,128)S(1)}, u32[]{:S(2)}, u32[]{:S(2)}) collective-permute-start(f32[7,64,128]{2,1,0:T(8,128)S(1)} %get-tuple-element.79), channel_id=1, source_target_pairs={{0,32},{32,0},{64,96},{96,64},{128,160},{160,128},{192,224},{224,1... | collective-permute-start | bytes 688136 | tf_op jit(solution)/shard_map/ppermute | solution.py:572
  41.6 1.2 collective-permute-start.10
  42.8 1.1 collective-permute-start.11
  43.8 2.0 %collective-permute-start.12 = (f32[7,64,128]{2,1,0:T(8,128)S(1)}, f32[7,64,128]{2,1,0:T(8,128)S(1)}, u32[]{:S(2)}, u32[]{:S(2)}) collective-permute-start(f32[7,64,128]{2,1,0:T(8,128)S(1)} %get-tuple-element.82), channel_id=1, source_target_pairs={{0,128},{32,160},{64,192},{96,224},{128,0},{160,32},{192,64},{224,... | collective-permute-start | bytes 688136 | tf_op jit(solution)/shard_map/ppermute | solution.py:572
  45.9 0.9 collective-permute-start.13
  46.8 0.0 collective-permute-done.9.refs_1_
  46.8 3.4 %collective-permute-start.14 = (f32[7,64,128]{2,1,0:T(8,128)S(1)}, f32[7,64,128]{2,1,0:T(8,128)S(1)}, u32[]{:S(2)}, u32[]{:S(2)}) collective-permute-start(f32[7,64,128]{2,1,0:T(8,128)S(1)} %get-tuple-element.84), channel_id=1, source_target_pairs={{0,192},{32,224},{64,0},{96,32},{128,64},{160,96},{192,128},{224,1... | collective-permute-start | bytes 688136 | tf_op jit(solution)/shard_map/ppermute | solution.py:572
  50.2 9.0 %collective-permute-start.15 = (f32[7,64,128]{2,1,0:T(8,128)S(1)}, f32[7,64,128]{2,1,0:T(8,128)S(1)}, u32[]{:S(2)}, u32[]{:S(2)}) collective-permute-start(f32[7,64,128]{2,1,0:T(8,128)S(1)} %get-tuple-element.85), channel_id=1, source_target_pairs={{0,224},{32,192},{64,32},{96,0},{128,96},{160,64},{192,160},{224,1... | collective-permute-start | bytes 688136 | tf_op jit(solution)/shard_map/ppermute | solution.py:572
  59.2 6.4 %collective-permute-done.12.refs_4_ = f32[7,64,128]{2,1,0:T(8,128)S(1)} collective-permute-done((f32[7,64,128]{2,1,0:T(8,128)S(1)}, f32[7,64,128]{2,1,0:T(8,128)S(1)}, u32[]{:S(2)}, u32[]{:S(2)}) %collective-permute-start.12) | collective-permute-done | bytes 229408 | tf_op jit(solution)/shard_map/ppermute | solution.py:572
  65.6 0.0 collective-permute-done.14.refs_6_
  65.6 0.0 collective-permute-done.15.refs_7_
  65.6 0.5 shard_map.32
  66.2 2.8 %collective-permute-start.16 = (f32[14,32,128]{2,1,0:T(8,128)S(1)}, f32[14,32,128]{2,1,0:T(8,128)S(1)}, u32[]{:S(2)}, u32[]{:S(2)}) collective-permute-start(f32[14,32,128]{2,1,0:T(8,128)S(1)} %get-tuple-element.88), channel_id=1, source_target_pairs={{0,2},{2,0},{4,6},{6,4},{8,10},{10,8},{12,14},{14,12},{16,18},{18,... | collective-permute-start | bytes 688136 | tf_op jit(solution)/shard_map/ppermute | solution.py:545
  69.0 1.3 %collective-permute-start.17 = (f32[2,32,128]{2,1,0:T(8,128)S(1)}, f32[2,32,128]{2,1,0:T(8,128)S(1)}, u32[]{:S(2)}, u32[]{:S(2)}) collective-permute-start(f32[2,32,128]{2,1,0:T(8,128)S(1)} %get-tuple-element.91), channel_id=1, source_target_pairs={{4,0},{6,2},{8,4},{10,6},{12,8},{14,10},{16,12},{18,14},{20,16},{2... | collective-permute-start | bytes 98312 | tf_op jit(solution)/shard_map/ppermute | solution.py:549
  70.3 3.9 %collective-permute-done.17.ends_ref = f32[2,32,128]{2,1,0:T(8,128)S(1)} collective-permute-done((f32[2,32,128]{2,1,0:T(8,128)S(1)}, f32[2,32,128]{2,1,0:T(8,128)S(1)}, u32[]{:S(2)}, u32[]{:S(2)}) %collective-permute-start.17) | collective-permute-done | bytes 32800 | tf_op jit(solution)/shard_map/ppermute | solution.py:549
  74.2 3.5 %collective-permute-start.18 = (f32[1,32,128]{2,1,0:T(8,128)S(1)}, f32[1,32,128]{2,1,0:T(8,128)S(1)}, u32[]{:S(2)}, u32[]{:S(2)}) collective-permute-start(f32[1,32,128]{2,1,0:T(8,128)S(1)} %get-tuple-element.93), channel_id=1, source_target_pairs={{0,4},{2,6},{4,8},{6,10},{8,12},{10,14},{12,16},{14,18},{16,20},{1... | collective-permute-start | bytes 49160 | tf_op jit(solution)/shard_map/ppermute | solution.py:549
  77.7 0.5 shard_map.33
  78.2 0.3 collective-permute-done.18.edge_ref
  78.6 0.1 shard_map.35
  78.7 18.2 %all_to_all.10.rhs_ref = f32[8,16,4,128]{3,2,1,0:T(4,128)S(1)} all-to-all(f32[8,16,4,128]{3,2,1,0:T(4,128)S(1)} %get-tuple-element.94), channel_id=1, replica_groups={{0,4,8,12,16,20,24,28},{2,6,10,14,18,22,26,30},{1,5,9,13,17,21,25,29},{..., dimensions={0} | all-to-all | bytes 524288 | tf_op jit(solution)/shard_map/all_to_all | solution.py:528
  96.8 0.1 shard_map.36
  96.9 11.4 %all_to_all.11.solved_ref = f32[8,14,4,128]{3,2,1,0:T(4,128)S(1)} all-to-all(f32[8,14,4,128]{3,2,1,0:T(4,128)S(1)} %shard_map.36), channel_id=1, replica_groups={{0,4,8,12,16,20,24,28},{2,6,10,14,18,22,26,30},{1,5,9,13,17,21,25,29},{..., dimensions={0} | all-to-all | bytes 458752 | tf_op jit(solution)/shard_map/all_to_all | solution.py:528
  108.3 0.1 shard_map.37
  108.4 4.9 %collective-permute-start.19 = (f32[14,32,128]{2,1,0:T(8,128)S(1)}, f32[14,32,128]{2,1,0:T(8,128)S(1)}, u32[]{:S(2)}, u32[]{:S(2)}) collective-permute-start(f32[14,32,128]{2,1,0:T(8,128)S(1)} %get-tuple-element.96), channel_id=1, source_target_pairs={{0,2},{2,0},{4,6},{6,4},{8,10},{10,8},{12,14},{14,12},{16,18},{18,... | collective-permute-start | bytes 688136 | tf_op jit(solution)/shard_map/ppermute | solution.py:545
  113.3 1.3 %shard_map.38.refs_0_ = f32[1,7,8,64,128]{4,3,2,1,0:T(8,128)} custom-call(f32[1,7,8,64,128]{4,3,2,1,0:T(8,128)S(1)} %copy-done, f32[7,64,128]{2,1,0:T(8,128)S(1)} %get-tuple-element.53.v_ref, f32[7,64,128]{2,1,0:T(8,128)S(1)} %get-tuple-element.54.w_ref, f32[7,7,32,128]{3,2,1,0:T(8,128)S(1)} %get-tuple-element.97.y_ref, ...), custom_call_target="tpu_custom_call" | custom-call | flops 917504 | bytes 2752512 | tf_op jit(solution)/shard_map/pallas_call | solution.py:489
  114.6 1.3 %shard_map.39 = f32[1,7,8,64,128]{4,3,2,1,0:T(8,128)} custom-call(f32[1,7,8,64,128]{4,3,2,1,0:T(8,128)S(1)} %copy-done, f32[7,64,128]{2,1,0:T(8,128)S(1)} %get-tuple-element.53.v_ref, f32[7,64,128]{2,1,0:T(8,128)S(1)} %get-tuple-element.54.w_ref, f32[7,7,32,128]{3,2,1,0:T(8,128)S(1)} %get-tuple-element.86.y_ref, ...), custom_call_target="tpu_custom_call", output_to_operand_aliasing={{}: (5, {})} | custom-call | flops 917504 | bytes 2752512 | tf_op jit(solution)/shard_map/pallas_call | solution.py:489
  (12 shorter events, 0.1 us)
Async XLA Ops:
  0.0 7.9 %copy-start = (f32[1,7,8,64,128]{4,3,2,1,0:T(8,128)S(1)}, f32[1,7,8,64,128]{4,3,2,1,0:T(8,128)}, u32[]{:S(2)}) copy-start(f32[1,7,8,64,128]{4,3,2,1,0:T(8,128)} %state_ref.7) | copy-start | bytes 5505028
  0.0 7.1 %copy-start.1 = (s32[1,8,64]{2,1,0:T(8,128)S(1)}, s32[1,8,64]{2,1,0:T(8,128)}, u32[]{:S(2)}) copy-start(s32[1,8,64]{2,1,0:T(8,128)} %flag_ref.1) | copy-start | bytes 6148
  1.8 6.0 %collective-permute-start = (f32[8,8,4,128]{3,2,1,0:T(4,128)S(1)}, f32[8,8,4,128]{3,2,1,0:T(4,128)S(1)}, u32[]{:S(2)}, u32[]{:S(2)}) collective-permute-start(f32[8,8,4,128]{3,2,1,0:T(4,128)S(1)} %get-tuple-element.52), channel_id=1, source_target_pairs={{0,1},{1,0},{2,3},{3,2},{4,5},{5,4},{6,7},{7,6},{8,9},{9,8},{10,11... | collective-permute-start | bytes 393224 | tf_op jit(solution)/shard_map/ppermute | solution.py:554
  5.4 13.5 %collective-permute-start.1 = (f32[7,64,128]{2,1,0:T(8,128)S(1)}, f32[7,64,128]{2,1,0:T(8,128)S(1)}, u32[]{:S(2)}, u32[]{:S(2)}) collective-permute-start(f32[7,64,128]{2,1,0:T(8,128)S(1)} %get-tuple-element.56), channel_id=1, source_target_pairs={{0,32},{32,0},{64,96},{96,64},{128,160},{160,128},{192,224},{224,1... | collective-permute-start | bytes 688136 | tf_op jit(solution)/shard_map/ppermute | solution.py:559
  5.8 16.5 %collective-permute-start.2 = (f32[7,64,128]{2,1,0:T(8,128)S(1)}, f32[7,64,128]{2,1,0:T(8,128)S(1)}, u32[]{:S(2)}, u32[]{:S(2)}) collective-permute-start(f32[7,64,128]{2,1,0:T(8,128)S(1)} %get-tuple-element.57), channel_id=1, source_target_pairs={{0,64},{32,96},{64,128},{96,160},{128,192},{160,224},{192,0},{224,... | collective-permute-start | bytes 688136 | tf_op jit(solution)/shard_map/ppermute | solution.py:559
  10.4 8.4 %collective-permute-start.8 = (f32[5,32,128]{2,1,0:T(8,128)S(1)}, f32[5,32,128]{2,1,0:T(8,128)S(1)}, u32[]{:S(2)}, u32[]{:S(2)}) collective-permute-start(f32[5,32,128]{2,1,0:T(8,128)S(1)} %get-tuple-element.65), channel_id=1, source_target_pairs={{0,2},{2,0},{4,6},{6,4},{8,10},{10,8},{12,14},{14,12},{16,18},{18,... | collective-permute-start | bytes 245768 | tf_op jit(solution)/shard_map/ppermute | solution.py:545
  15.7 9.3 %collective-permute-start.3 = (f32[7,64,128]{2,1,0:T(8,128)S(1)}, f32[7,64,128]{2,1,0:T(8,128)S(1)}, u32[]{:S(2)}, u32[]{:S(2)}) collective-permute-start(f32[7,64,128]{2,1,0:T(8,128)S(1)} %get-tuple-element.58), channel_id=1, source_target_pairs={{0,96},{32,64},{64,160},{96,128},{128,224},{160,192},{192,32},{224... | collective-permute-start | bytes 688136 | tf_op jit(solution)/shard_map/ppermute | solution.py:559
  16.2 18.9 %collective-permute-start.4 = (f32[7,64,128]{2,1,0:T(8,128)S(1)}, f32[7,64,128]{2,1,0:T(8,128)S(1)}, u32[]{:S(2)}, u32[]{:S(2)}) collective-permute-start(f32[7,64,128]{2,1,0:T(8,128)S(1)} %get-tuple-element.59), channel_id=1, source_target_pairs={{0,128},{32,160},{64,192},{96,224},{128,0},{160,32},{192,64},{224,... | collective-permute-start | bytes 688136 | tf_op jit(solution)/shard_map/ppermute | solution.py:559
  18.8 16.3 %collective-permute-start.5 = (f32[7,64,128]{2,1,0:T(8,128)S(1)}, f32[7,64,128]{2,1,0:T(8,128)S(1)}, u32[]{:S(2)}, u32[]{:S(2)}) collective-permute-start(f32[7,64,128]{2,1,0:T(8,128)S(1)} %get-tuple-element.60), channel_id=1, source_target_pairs={{0,160},{32,128},{64,224},{96,192},{128,32},{160,0},{192,96},{224,... | collective-permute-start | bytes 688136 | tf_op jit(solution)/shard_map/ppermute | solution.py:559
  19.0 19.2 %collective-permute-start.6 = (f32[7,64,128]{2,1,0:T(8,128)S(1)}, f32[7,64,128]{2,1,0:T(8,128)S(1)}, u32[]{:S(2)}, u32[]{:S(2)}) collective-permute-start(f32[7,64,128]{2,1,0:T(8,128)S(1)} %get-tuple-element.61), channel_id=1, source_target_pairs={{0,192},{32,224},{64,0},{96,32},{128,64},{160,96},{192,128},{224,1... | collective-permute-start | bytes 688136 | tf_op jit(solution)/shard_map/ppermute | solution.py:559
  22.2 16.0 %collective-permute-start.7 = (f32[7,64,128]{2,1,0:T(8,128)S(1)}, f32[7,64,128]{2,1,0:T(8,128)S(1)}, u32[]{:S(2)}, u32[]{:S(2)}) collective-permute-start(f32[7,64,128]{2,1,0:T(8,128)S(1)} %get-tuple-element.62), channel_id=1, source_target_pairs={{0,224},{32,192},{64,32},{96,0},{128,96},{160,64},{192,160},{224,1... | collective-permute-start | bytes 688136 | tf_op jit(solution)/shard_map/ppermute | solution.py:559
  39.5 7.3 %collective-permute-start.9 = (f32[7,64,128]{2,1,0:T(8,128)S(1)}, f32[7,64,128]{2,1,0:T(8,128)S(1)}, u32[]{:S(2)}, u32[]{:S(2)}) collective-permute-start(f32[7,64,128]{2,1,0:T(8,128)S(1)} %get-tuple-element.79), channel_id=1, source_target_pairs={{0,32},{32,0},{64,96},{96,64},{128,160},{160,128},{192,224},{224,1... | collective-permute-start | bytes 688136 | tf_op jit(solution)/shard_map/ppermute | solution.py:572
  41.6 8.6 %collective-permute-start.10 = (f32[7,64,128]{2,1,0:T(8,128)S(1)}, f32[7,64,128]{2,1,0:T(8,128)S(1)}, u32[]{:S(2)}, u32[]{:S(2)}) collective-permute-start(f32[7,64,128]{2,1,0:T(8,128)S(1)} %get-tuple-element.80), channel_id=1, source_target_pairs={{0,64},{32,96},{64,128},{96,160},{128,192},{160,224},{192,0},{224,... | collective-permute-start | bytes 688136 | tf_op jit(solution)/shard_map/ppermute | solution.py:572
  42.8 16.4 %collective-permute-start.11 = (f32[7,64,128]{2,1,0:T(8,128)S(1)}, f32[7,64,128]{2,1,0:T(8,128)S(1)}, u32[]{:S(2)}, u32[]{:S(2)}) collective-permute-start(f32[7,64,128]{2,1,0:T(8,128)S(1)} %get-tuple-element.81), channel_id=1, source_target_pairs={{0,96},{32,64},{64,160},{96,128},{128,224},{160,192},{192,32},{224... | collective-permute-start | bytes 688136 | tf_op jit(solution)/shard_map/ppermute | solution.py:572
  43.8 21.8 %collective-permute-start.12 = (f32[7,64,128]{2,1,0:T(8,128)S(1)}, f32[7,64,128]{2,1,0:T(8,128)S(1)}, u32[]{:S(2)}, u32[]{:S(2)}) collective-permute-start(f32[7,64,128]{2,1,0:T(8,128)S(1)} %get-tuple-element.82), channel_id=1, source_target_pairs={{0,128},{32,160},{64,192},{96,224},{128,0},{160,32},{192,64},{224,... | collective-permute-start | bytes 688136 | tf_op jit(solution)/shard_map/ppermute | solution.py:572
  45.9 19.7 %collective-permute-start.13 = (f32[7,64,128]{2,1,0:T(8,128)S(1)}, f32[7,64,128]{2,1,0:T(8,128)S(1)}, u32[]{:S(2)}, u32[]{:S(2)}) collective-permute-start(f32[7,64,128]{2,1,0:T(8,128)S(1)} %get-tuple-element.83), channel_id=1, source_target_pairs={{0,160},{32,128},{64,224},{96,192},{128,32},{160,0},{192,96},{224,... | collective-permute-start | bytes 688136 | tf_op jit(solution)/shard_map/ppermute | solution.py:572
  46.8 18.8 %collective-permute-start.14 = (f32[7,64,128]{2,1,0:T(8,128)S(1)}, f32[7,64,128]{2,1,0:T(8,128)S(1)}, u32[]{:S(2)}, u32[]{:S(2)}) collective-permute-start(f32[7,64,128]{2,1,0:T(8,128)S(1)} %get-tuple-element.84), channel_id=1, source_target_pairs={{0,192},{32,224},{64,0},{96,32},{128,64},{160,96},{192,128},{224,1... | collective-permute-start | bytes 688136 | tf_op jit(solution)/shard_map/ppermute | solution.py:572
  50.2 15.4 %collective-permute-start.15 = (f32[7,64,128]{2,1,0:T(8,128)S(1)}, f32[7,64,128]{2,1,0:T(8,128)S(1)}, u32[]{:S(2)}, u32[]{:S(2)}) collective-permute-start(f32[7,64,128]{2,1,0:T(8,128)S(1)} %get-tuple-element.85), channel_id=1, source_target_pairs={{0,224},{32,192},{64,32},{96,0},{128,96},{160,64},{192,160},{224,1... | collective-permute-start | bytes 688136 | tf_op jit(solution)/shard_map/ppermute | solution.py:572
  66.2 12.4 %collective-permute-start.16 = (f32[14,32,128]{2,1,0:T(8,128)S(1)}, f32[14,32,128]{2,1,0:T(8,128)S(1)}, u32[]{:S(2)}, u32[]{:S(2)}) collective-permute-start(f32[14,32,128]{2,1,0:T(8,128)S(1)} %get-tuple-element.88), channel_id=1, source_target_pairs={{0,2},{2,0},{4,6},{6,4},{8,10},{10,8},{12,14},{14,12},{16,18},{18,... | collective-permute-start | bytes 688136 | tf_op jit(solution)/shard_map/ppermute | solution.py:545
  69.0 5.2 %collective-permute-start.17 = (f32[2,32,128]{2,1,0:T(8,128)S(1)}, f32[2,32,128]{2,1,0:T(8,128)S(1)}, u32[]{:S(2)}, u32[]{:S(2)}) collective-permute-start(f32[2,32,128]{2,1,0:T(8,128)S(1)} %get-tuple-element.91), channel_id=1, source_target_pairs={{4,0},{6,2},{8,4},{10,6},{12,8},{14,10},{16,12},{18,14},{20,16},{2... | collective-permute-start | bytes 98312 | tf_op jit(solution)/shard_map/ppermute | solution.py:549
  74.2 4.4 %collective-permute-start.18 = (f32[1,32,128]{2,1,0:T(8,128)S(1)}, f32[1,32,128]{2,1,0:T(8,128)S(1)}, u32[]{:S(2)}, u32[]{:S(2)}) collective-permute-start(f32[1,32,128]{2,1,0:T(8,128)S(1)} %get-tuple-element.93), channel_id=1, source_target_pairs={{0,4},{2,6},{4,8},{6,10},{8,12},{10,14},{12,16},{14,18},{16,20},{1... | collective-permute-start | bytes 49160 | tf_op jit(solution)/shard_map/ppermute | solution.py:549
  108.4 6.2 %collective-permute-start.19 = (f32[14,32,128]{2,1,0:T(8,128)S(1)}, f32[14,32,128]{2,1,0:T(8,128)S(1)}, u32[]{:S(2)}, u32[]{:S(2)}) collective-permute-start(f32[14,32,128]{2,1,0:T(8,128)S(1)} %get-tuple-element.96), channel_id=1, source_target_pairs={{0,2},{2,0},{4,6},{6,4},{8,10},{10,8},{12,14},{14,12},{16,18},{18,... | collective-permute-start | bytes 688136 | tf_op jit(solution)/shard_map/ppermute | solution.py:545
